TPU v7x, 32 devices: a whole 2x2x4 slice. The times are simulated.
32 devices in a mesh: wide: 16 (over z, y, core), narrow: 2 (over x).
Axes of the slice: x: 2, y: 2, z: 4, core: 2. Of those that a mesh axis runs over, the one named last changes fastest.
Arguments:
- frames_in: bfloat16 [32, 256, 1152], P(('wide', 'narrow')), may hold values from -6 to 6
- conditioning: bfloat16 [32, 1152], P(('wide', 'narrow')), may hold values from -5 to 5
- grid: int32 [32, 2], P(('wide', 'narrow')), may hold values from 8 to 32, as said below
- cotangent: bfloat16 [32, 256, 1152], P(('wide', 'narrow')), may hold values from -6 to 6
- mod_weight: float32 [1152, 6912], P(('wide', 'narrow')), may hold values from -0.1875 to 0.1875
- qkv_weight: float32 [1152, 3456], P(('wide', 'narrow')), may hold values from -0.1875 to 0.1875
- out_weight: float32 [1152, 1152], P(('wide', 'narrow')), may hold values from -1 to 1
- up_weight: float32 [1152, 4608], P(('wide', 'narrow')), may hold values from -0.1875 to 0.1875
- down_weight: float32 [4608, 1152], P(('wide', 'narrow')), may hold values from -0.09375 to 0.09375
- biases: float32 [16128], P(('wide', 'narrow')), may hold values from -1.2 to 1.2
- mod_state: float32 [3, 1152, 6912], P(None, ('wide', 'narrow')), as said below
- qkv_state: float32 [3, 1152, 3456], P(None, ('wide', 'narrow')), as said below
- out_state: float32 [3, 1152, 1152], P(None, ('wide', 'narrow')), as said below
- up_state: float32 [3, 1152, 4608], P(None, ('wide', 'narrow')), as said below
- down_state: float32 [3, 4608, 1152], P(None, ('wide', 'narrow')), as said below
- bias_state: float32 [3, 16128], P(None, ('wide', 'narrow')), as said below
Outputs:
- block_out: bfloat16 [32, 256, 1152], P(('wide', 'narrow'))
- frames_grad: bfloat16 [32, 256, 1152], P(('wide', 'narrow'))
- cond_grad: float32 [32, 1152], P(('wide', 'narrow'))
- grad_norm: float32 [], replicated
- mod_grad: float32 [1152, 6912], P(('wide', 'narrow'))
- qkv_grad: float32 [1152, 3456], P(('wide', 'narrow'))
- out_grad: float32 [1152, 1152], P(('wide', 'narrow'))
- up_grad: float32 [1152, 4608], P(('wide', 'narrow'))
- down_grad: float32 [4608, 1152], P(('wide', 'narrow'))
- bias_grad: float32 [16128], P(('wide', 'narrow'))
- mod_new: float32 [1152, 6912], P(('wide', 'narrow'))
- qkv_new: float32 [1152, 3456], P(('wide', 'narrow'))
- out_new: float32 [1152, 1152], P(('wide', 'narrow'))
- up_new: float32 [1152, 4608], P(('wide', 'narrow'))
- down_new: float32 [4608, 1152], P(('wide', 'narrow'))
- bias_new: float32 [16128], P(('wide', 'narrow'))
- mod_state_new: float32 [3, 1152, 6912], P(None, ('wide', 'narrow'))
- qkv_state_new: float32 [3, 1152, 3456], P(None, ('wide', 'narrow'))
- out_state_new: float32 [3, 1152, 1152], P(None, ('wide', 'narrow'))
- up_state_new: float32 [3, 1152, 4608], P(None, ('wide', 'narrow'))
- down_state_new: float32 [3, 4608, 1152], P(None, ('wide', 'narrow'))
- bias_state_new: float32 [3, 16128], P(None, ('wide', 'narrow'))
Inputs may be any that keep to these rules, and one draw needn't show every extreme that they name: Each frame's grid is (16, 16), (12, 20) or (8, 32); frame 0 has the first and frame 1 the last. `mod_state`: slot 0 holds first moments, slot 1 second moments (positive), slot 2 the weight average. `qkv_state`: slot 0 holds first moments, slot 1 second moments (positive), slot 2 the weight average. `out_state`: slot 0 holds first moments, slot 1 second moments (positive), slot 2 the weight average. `up_state`: slot 0 holds first moments, slot 1 second moments (positive), slot 2 the weight average. `down_state`: slot 0 holds first moments, slot 1 second moments (positive), slot 2 the weight average. `bias_state`: slot 0 holds first moments, slot 1 second moments (positive), slot 2 the weight average.
All inputs are finite; a program needn't handle non-finite values.
Results may differ from a plain program's by a relative error of at most 0.014.
The roundings to bfloat16 on the way count: a program that leaves them out, or rounds other values in their place, can miss the bound.
Values may be sent and summed in bfloat16 or wider, within the bound.
A program may use at most 384 MiB of HBM per device.

v0:
```python
import functools
import jax
import jax.numpy as jnp
from jax import lax
from jax.experimental import pallas as pl
from jax.experimental.pallas import tpu as pltpu
from jax.sharding import PartitionSpec as P

HEADS = 16
STEPS = 4
CLIP = 576
NORM_EPS = 1e-06
RATE = 0.04
FIRST_DECAY = 0.5
SECOND_DECAY = 0.5
WEIGHT_DECAY = 0.1
ADAM_EPS = 1e-08
AVERAGE_DECAY = 0.9999
MASK_VALUE = -1e30
AXES = ("wide", "narrow")

MESH = pl.DeviceIdType.MESH
CORE = 1
ROUND = 16


def orders(bits, late):
    high = list(range(bits - 1, 2, -1))
    if late:
        pair = (high[:-1] + [0, 2] + high[-1:], high[:-1] + [2, 0] + high[-1:])
    else:
        pair = (high + [2, 0], high + [0, 2])
    return tuple(order + [CORE] for order in pair)


def top_place(member):
    return member.bit_length() - 1


def quotient(value, by):
    return lax.div(value, jnp.int32(by))


def remainder(value, by):
    return lax.rem(value, jnp.int32(by))


class Spots:
    def __init__(self, bits):
        wide, narrow = lax.axis_index("wide"), lax.axis_index("narrow")
        self.bits = bits
        self.me = wide * 2 + narrow
        self.quad = remainder(self.me, 4)
        self.group = quotient(self.me, 4)
        self.digit = [remainder(quotient(self.me, 1 << bit), 2) for bit in range(bits)]
        self.core = self.digit[CORE]
        self.delta = [(1 << bit) * (1 - 2 * self.digit[bit]) for bit in range(bits)]
        self.device = [
            (wide, 1 - narrow) if bit == 0 else (wide + (1 << bit - 1) * (1 - 2 * self.digit[bit]), narrow)
            for bit in range(bits)
        ]
        self.steps = {}
        first = self.core == 0
        for late in (False, True):
            pair = orders(bits, late)
            own, other, devices = [], [], []
            for place in range(bits):
                zero, one = pair[0][place], pair[1][place]
                if zero == one:
                    own.append(self.delta[zero])
                    other.append(self.delta[zero])
                    devices.append(self.device[zero])
                else:
                    own.append(jnp.where(first, self.delta[zero], self.delta[one]))
                    other.append(jnp.where(first, self.delta[one], self.delta[zero]))
                    devices.append(
                        tuple(jnp.where(first, a, b) for a, b in zip(self.device[zero], self.device[one]))
                    )
            self.steps[late] = (own, other, devices)
        self.opposite = (self.device[CORE][0], self.device[0][1])

    def block(self, late, member):
        own, other, _ = self.steps[late]
        last = self.bits - 1
        table = other if member >> last & 1 else own
        index = self.me
        for place in range(self.bits):
            if member >> place & 1:
                index = index + table[place]
        return index

    def partner(self, late, place):
        return self.steps[late][2][place]

    def near(self, other):
        if other == 3:
            return self.opposite, 3 - self.quad
        bit = other - 1
        return self.device[bit], self.quad + self.delta[bit]

    def greet(self):
        barrier = pltpu.get_barrier_semaphore()
        partners = self.device + [self.opposite]
        for partner in partners:
            pl.semaphore_signal(barrier, inc=1, device_id=partner, device_id_type=MESH)
        pl.semaphore_wait(barrier, len(partners))


def remote(source, target, send_sem, recv_sem, device):
    copy = pltpu.make_async_remote_copy(
        src_ref=source, dst_ref=target, send_sem=send_sem, recv_sem=recv_sem, device_id=device, device_id_type=MESH
    )
    copy.start()
    return copy


def local(source, target, sem):
    copy = pltpu.make_async_copy(source, target, sem)
    copy.start()
    return copy


def await_bytes(spot, sem):
    pltpu.make_async_copy(spot, spot, sem).wait()


def aligned(start, size, by=16):
    return pl.ds(pl.multiple_of(start, by), size)


def repeat(times, body):
    def run(index, carry):
        body(index)
        return carry

    lax.fori_loop(0, times, run, 0)


class Agenda:
    def __init__(self):
        self.services = []
        self.steps = []
        self.now = 0.0

    def service(self, when, action):
        self.services.append((when, len(self.services), action))

    def step(self, takes, action, after=0.0):
        self.steps.append((takes, action, after))

    def emit(self):
        while self.services or self.steps:
            self.services.sort(key=lambda item: item[:2])
            due = self.services[0][0] if self.services else None
            after = self.steps[0][2] if self.steps else None
            if self.services and (not self.steps or due <= self.now or (after > self.now and due <= after)):
                when, _, action = self.services.pop(0)
                self.now = max(self.now, when) + 0.1
            else:
                takes, action, after = self.steps.pop(0)
                self.now = max(self.now, after) + takes
            action()


def nn(left, right):
    return jnp.dot(left, right, preferred_element_type=jnp.float32)


def nt(left, right):
    return lax.dot_general(left, right, (((1,), (1,)), ((), ())), preferred_element_type=jnp.float32)


def tn(left, right):
    return lax.dot_general(left, right, (((0,), (0,)), ((), ())), preferred_element_type=jnp.float32)


def gelu_parts(value):
    bend = jnp.tanh(0.7978845608028654 * (value + 0.044715 * value * value * value))
    slope = 0.7978845608028654 * (1.0 + 0.134145 * value * value)
    return 0.5 * value * (1.0 + bend), 0.5 * (1.0 + bend) + 0.5 * value * (1.0 - bend * bend) * slope


def normalized(value):
    centre = jnp.mean(value, axis=-1, keepdims=True)
    centred = value - centre
    spread = jnp.mean(centred * centred, axis=-1, keepdims=True)
    root = lax.rsqrt(spread + NORM_EPS)
    return centred * root, root


def head_window(head, size):
    first, last = head * size // 128, (head * size + size - 1) // 128
    return first * 128, (last + 1 - first) * 128, head * size - first * 128


def only_head(values, offset, size):
    lane = lax.broadcasted_iota(jnp.int32, values.shape, 1)
    return jnp.where(jnp.logical_and(lane >= offset, lane < offset + size), values, jnp.zeros((), values.dtype))


STRIP = 32
TILE = 384


def forward_kernel(bits, rows, pieces, clock,
                   a_src, b_src, c_src, terms_in, mod_bias, bias_rows, frames, cot, key_mask, row_mask,
                   a_out, b_out, c_out, mod_out, query_out, key_out, value_out, total_out,
                   branch_out, midway_out, slope_out, active_out, change_out, turned_out, down_out, bias_out,
                   stage, block, c_block, terms, landed, x_ref, first, query, key, value, totals, joined, attended,
                   branch, midway, second, active, active_turned, other_turned, change, other_change, turned,
                   weight, slope_stage, down_stage,
                   quad_send, quad_recv, own_sem, keep_sem, send_sem, recv_sem, term_send, term_recv,
                   pair_send, pair_recv, load_sem, weight_sem, save_sem, slope_sem, down_sem):
    count = 1 << bits
    spots = Spots(bits)
    quad, core = spots.quad, spots.core
    sibling = spots.device[CORE]
    outs = (a_out, b_out, c_out)
    tall_rows = c_src.shape[0]
    tokens, width = first.shape
    size = width // HEADS
    scale = size ** (-0.5)
    low = jnp.bfloat16
    finals = []

    def save(source, target, index):
        finals.append(local(source, target, save_sem.at[index]).wait)

    def place(piece, index):
        kind, start, length, _ = pieces[piece]
        if kind == 2:
            return c_out.at[aligned(index * tall_rows + start, length)]
        return outs[kind].at[remainder(index, 4), aligned(quotient(index, 4) * (4 * rows) + start, length)]

    def of_kind(kind):
        return [piece for piece, entry in enumerate(pieces) if entry[0] == kind]

    own = [local(source.at[quad], stage.at[kind, quad], own_sem.at[kind]) for kind, source in enumerate((a_src, b_src))]
    own.append(local(c_src, c_block, own_sem.at[2]))
    loads = [local(terms_in, terms, load_sem.at[0]), local(frames, x_ref, load_sem.at[1])]
    spots.greet()
    quads = []

    def start_quad(kind, source):
        for other in (1, 2, 3):
            device, spot = spots.near(other)
            copy = remote(source.at[spot], stage.at[kind, quad], quad_send.at[kind, other], quad_recv.at[kind, other], device)
            quads.append(copy)
            finals.append(copy.wait_send)

    keeps = {}

    def launch(piece, member, source):
        late = pieces[piece][3]
        spot = spots.block(late, member)
        for step in range(top_place(member) + 1, bits):
            target = member | 1 << step
            copy = remote(
                source, place(piece, spot), send_sem.at[piece, target], recv_sem.at[piece, target], spots.partner(late, step)
            )
            finals.append(copy.wait_send)

    def open_pieces(kind, source):
        for piece in of_kind(kind):
            _, start, length, _ = pieces[piece]
            part = source.at[pl.ds(start, length)]
            launch(piece, 0, part)
            keeps[piece] = local(part, place(piece, spots.me), keep_sem.at[piece])

    def arrived(piece, member):
        spot = place(piece, spots.block(pieces[piece][3], member))
        await_bytes(spot, recv_sem.at[piece, member])
        return spot

    def open_quad(kind):
        own[kind].wait()
        for copy in quads[3 * kind : 3 * kind + 3]:
            copy.wait_recv()
        for lane in range(0, width, 128):
            parts = [stage[kind, q, :, lane : lane + 128].astype(jnp.float32) for q in range(4)]
            block[kind, :, lane : lane + 128] = jnp.concatenate(parts, axis=0).astype(low)
        open_pieces(kind, block.at[kind])

    crossed = [CORE, 0] + list(range(2, bits))
    term_copies = []

    def start_term(step):
        given = tuple(spots.digit[bit] for bit in crossed[:step]) + (1 - spots.digit[crossed[step]],)
        copy = remote(terms.at[given], landed[step], term_send.at[step], term_recv.at[step], spots.device[crossed[step]])
        term_copies.append(copy)
        finals.append(copy.wait_send)

    def end_term(step):
        kept = tuple(spots.digit[bit] for bit in crossed[: step + 1])
        term_copies[step].wait_recv()
        terms[kept] = terms[kept] + landed[step][...]
        if step + 1 < bits:
            start_term(step + 1)
            return
        parts = terms[kept] + mod_bias[...]
        per = width // 128
        for at in range(6 * per):
            part, lane = at // per, at % per * 128
            mod_out[part : part + 1, lane : lane + 128] = parts[at : at + 1, :]

    start_quad(0, a_src)
    loads[0].wait()
    start_term(0)
    own[2].wait()
    open_pieces(2, c_block)
    open_quad(0)
    start_quad(1, b_src)
    open_quad(1)
    agenda = Agenda()
    for step in range(bits):
        agenda.service(clock["terms"][0] + clock["terms"][1] * step, functools.partial(end_term, step))
    full = [0.0] * 3
    for piece, (kind, _, _, _) in enumerate(pieces):
        begin, pace = clock["pieces"][piece]
        for member in range(1, count // 2):
            agenda.service(
                begin + pace * member,
                lambda piece=piece, member=member: launch(piece, member, arrived(piece, member)),
            )
        full[kind] = max(full[kind], begin + pace * (count // 2) + clock["settle"])

    def finish(kind):
        for piece in of_kind(kind):
            for member in range(count // 2, count):
                arrived(piece, member)
            keeps[piece].wait()

    def load_weight(kind, q, slot):
        return local(outs[kind].at[q], weight.at[slot], weight_sem.at[slot])

    def over_strips(body):
        repeat(tokens // STRIP, lambda s: body(aligned(s * STRIP, STRIP, STRIP)))

    def over_tiles(body):
        repeat(width // TILE, lambda t: body(aligned(t * TILE, TILE, 128)))

    pairs = {}

    def trade(index, source, target):
        pairs[index] = remote(source, target, pair_send.at[index], pair_recv.at[index], sibling)
        finals.append(pairs[index].wait_send)

    def turn(source, index):
        repeat(
            width // 128,
            lambda t: turned.__setitem__(
                (index, aligned(t * 128, 128, 128)), source[:, aligned(t * 128, 128, 128)].T
            ),
        )
        save(turned.at[index], turned_out.at[index, 0], 8 + index)
        trade(index, turned.at[index], turned_out.at[index, 1])
        finals.append(pairs[index].wait_recv)

    def norm_first():
        loads[1].wait()

        def body(where):
            unit, _ = normalized(x_ref[where, :].astype(jnp.float32))
            first[where, :] = (unit * (1.0 + mod_out[1:2, :]) + mod_out[0:1, :]).astype(low)
            upstream = cot[where, :].astype(jnp.float32) * row_mask[where, :]
            change[where, :] = (mod_out[5:6, :] * upstream).astype(low)

        over_strips(body)
        save(change, change_out, 0)
        trade(3, change, other_change)
        bias_out[...] = jnp.zeros_like(bias_out)
        bias_out[0:1, :] = jnp.sum(change[...].astype(jnp.float32), axis=0, keepdims=True)

    weight_loads = {}

    def begin_first():
        finish(0)
        for s in range(2):
            weight_loads[s] = load_weight(0, s, s)

    def project(s, target, bias):
        slot = s % 2
        weight_loads[s].wait()

        def body(where):
            result = nn(first[...], weight[slot, :, where])
            if bias is not None:
                result = result + bias_rows[bias : bias + 1, where]
            target[:, where] = result.astype(low)

        over_tiles(body)
        if s + 2 < 4:
            weight_loads[s + 2] = load_weight(0, s + 2, slot)
        save(target, (query_out, key_out, value_out)[s], 1 + s)

    def clear():
        joined[...] = jnp.zeros_like(joined)
        totals[...] = jnp.zeros_like(totals)

    def attend(head):
        start, span, offset = head_window(head, size)
        where = slice(start, start + span)
        scores = nt(only_head(query[:, where], offset, size), key[:, where])
        scores = jnp.where(key_mask[0:1, :] > 0, scores * scale, MASK_VALUE)
        peak = jnp.max(scores, axis=-1, keepdims=True)
        power = jnp.exp(scores - peak)
        total = jnp.sum(power, axis=-1, keepdims=True)
        attention = (power / total).astype(low)
        joined[:, where] = joined[:, where] + nn(attention, only_head(value[:, where], offset, size))
        lane = lax.broadcasted_iota(jnp.int32, (tokens, 128), 1)
        totals[...] = jnp.where(lane == head, peak + jnp.log(total), totals[...])

    def leave_attention():
        attended[...] = joined[...].astype(low)
        save(totals, total_out, 4)
        weight_loads[3].wait()

        def body(where):
            result = nn(attended[...], weight[1, :, where]) + bias_rows[2:3, where]
            branch[:, where] = result
            midway[:, where] = x_ref[:, where].astype(jnp.float32) + mod_out[2:3, where] * result

        over_tiles(body)
        save(branch, branch_out, 5)
        save(midway, midway_out, 6)

    def norm_second():
        def body(where):
            unit, _ = normalized(midway[where, :])
            second[where, :] = (unit * (1.0 + mod_out[4:5, :]) + mod_out[3:4, :]).astype(low)

        over_strips(body)

    up_loads = {}
    slope_copies = {}

    def begin_up():
        finish(1)
        for s in range(2):
            up_loads[s] = load_weight(1, s, s)

    def raise_up(s):
        slot = s % 2
        up_loads[s].wait()
        if s >= 2:
            slope_copies[s - 2].wait()

        def body(t):
            where = aligned(t * TILE, TILE, 128)
            wide = aligned(s * width + t * TILE, TILE, 128)
            bent, slope = gelu_parts(nn(second[...], weight[slot, :, where]) + bias_rows[aligned(3 + s, 1, 1), where])
            active[:, wide] = bent.astype(low)
            active_turned[wide, :] = bent.astype(low).T
            slope_stage[slot, :, where] = slope

        repeat(width // TILE, body)
        if s + 2 < 4:
            up_loads[s + 2] = load_weight(1, s + 2, slot)
        slope_copies[s] = local(
            slope_stage.at[slot], slope_out.at[:, pl.ds(s * width, width)], slope_sem.at[slot]
        )

    span = 2 * tall_rows

    def plane_rows(j, plane):
        return aligned((2 * j + plane) * span, span)

    def trade_active():
        save(active, active_out, 7)
        for j in range(count // 4):
            trade(4 + j, active_turned.at[plane_rows(j, 1 - core)], other_turned.at[pl.ds(j * span, span)])

    down_copies = {}

    def down_gradient(j):
        slot = j % 2
        if j == 0:
            pairs[3].wait_recv()
        if j >= 2:
            down_copies[j - 2].wait()
        pairs[4 + j].wait_recv()

        def body(where):
            result = nn(active_turned[plane_rows(j, core), :], change[:, where])
            result = result + nn(other_turned[j * span : (j + 1) * span, :], other_change[:, where])
            down_stage[slot, :, where] = result.astype(low)

        over_tiles(body)
        down_copies[j] = local(down_stage.at[slot], down_out.at[pl.ds(j * span, span)], down_sem.at[slot])

    takes = clock["takes"]
    agenda.step(takes["norm"], norm_first, clock["terms"][0] + clock["terms"][1] * bits)
    agenda.step(takes["turn"], lambda: turn(first, 0))
    agenda.step(0.3, begin_first, full[0])
    for s, (target, bias) in enumerate(((query, 0), (key, None), (value, 1))):
        agenda.step(takes["matmul"], functools.partial(project, s, target, bias))
    agenda.step(0.3, clear)
    for head in range(HEADS):
        agenda.step(takes["head"], functools.partial(attend, head))
    agenda.step(takes["matmul"], leave_attention)
    agenda.step(takes["norm"], norm_second)
    agenda.step(0.3, begin_up, full[1])
    for s in range(4):
        agenda.step(takes["up"], functools.partial(raise_up, s))
    agenda.step(0.3, trade_active)
    agenda.step(takes["turn"], lambda: turn(attended, 1))
    agenda.step(takes["turn"], lambda: turn(second, 2))
    for j in range(count // 4):
        agenda.step(takes["down"], functools.partial(down_gradient, j))
    agenda.emit()
    finish(2)
    for done in finals:
        done()
    for table in (slope_copies, down_copies):
        for index in sorted(table)[-2:]:
            table[index].wait()


PIECES = ((0, 0, 96, False), (0, 96, 48, True), (1, 0, 96, False), (1, 96, 48, True), (2, 0, 96, False), (2, 96, 48, True))
CLOCK = {
    "terms": (12.0, 5.0),
    "pieces": ((8.0, 2.4), (8.0, 2.4), (16.0, 4.6), (16.0, 4.6), (24.0, 6.6), (24.0, 6.6)),
    "settle": 3.0,
    "takes": {"norm": 2.0, "turn": 0.6, "matmul": 2.0, "head": 0.8, "up": 3.5, "down": 1.2},
}


def forward(a_src, b_src, c_src, terms, mod_bias, bias_rows, frames, cot, key_mask, row_mask, pieces=PIECES, clock=CLOCK):
    rows, width = a_src.shape[1:]
    tall = c_src.shape[0]
    bits = terms.ndim - 2
    count = 1 << bits
    tokens = frames.shape[0]
    hidden = tall * count
    low, wide = jnp.bfloat16, jnp.float32

    def shaped(*sizes, dtype=low):
        return jax.ShapeDtypeStruct(sizes, dtype)

    anywhere = pl.BlockSpec(memory_space=pl.ANY)
    near = pl.BlockSpec(memory_space=pltpu.VMEM)
    token = shaped(tokens, width)
    token_wide = shaped(tokens, width, dtype=wide)
    outs = (
        shaped(4, width, width), shaped(4, width, width), shaped(hidden, width),
        shaped(8, width, dtype=wide),
        token, token, token, shaped(tokens, 128, dtype=wide),
        token_wide, token_wide,
        shaped(tokens, hidden, dtype=wide), shaped(tokens, hidden), token,
        shaped(3, 2, width, tokens),
        shaped(hidden // 2, width), shaped(8, width, dtype=wide),
    )
    out_specs = [anywhere] * len(outs)
    out_specs[3] = near
    out_specs[-1] = near
    dma = pltpu.SemaphoreType.DMA
    v = pltpu.VMEM
    scratch = [
        v((2, 4, rows, width), low), v((2, 4 * rows, width), low), v((tall, width), low),
        v(terms.shape, wide), tuple(v(terms.shape[step + 1 :], wide) for step in range(bits)),
        v((tokens, width), low), v((tokens, width), low),
        v((tokens, width), low), v((tokens, width), low), v((tokens, width), low),
        v((tokens, 128), wide), v((tokens, width), wide), v((tokens, width), low),
        v((tokens, width), wide), v((tokens, width), wide), v((tokens, width), low),
        v((tokens, hidden), low), v((hidden, tokens), low), v((hidden // 2, tokens), low),
        v((tokens, width), low), v((tokens, width), low), v((3, width, tokens), low),
        v((2, width, width), low), v((2, tokens, width), wide), v((2, 2 * tall, width), low),
        dma((2, 4)), dma((2, 4)), dma((3,)), dma((len(pieces),)), dma((len(pieces), count)), dma((len(pieces), count)),
        dma((bits,)), dma((bits,)), dma((4 + count // 4,)), dma((4 + count // 4,)),
        dma((2,)), dma((2,)), dma((16,)), dma((2,)), dma((2,)),
    ]
    return pl.pallas_call(
        functools.partial(forward_kernel, bits, rows, pieces, clock),
        out_shape=outs,
        in_specs=[anywhere] * 4 + [near] * 2 + [anywhere] + [near] * 3,
        out_specs=out_specs,
        scratch_shapes=scratch,
        compiler_params=pltpu.CompilerParams(collective_id=0, has_side_effects=True, vmem_limit_bytes=56 * 1024 * 1024),
        cost_estimate=pl.CostEstimate(flops=10_000_000_000, bytes_accessed=400_000_000, transcendentals=3_000_000),
        name="forward_gather",
    )(a_src, b_src, c_src, terms, mod_bias, bias_rows, frames, cot, key_mask, row_mask)


def SPREAD(bits):
    return list(range(bits - 1, 1, -1)) + [0, CORE]


def folded_rows(values):
    whole = values.shape[0] // 8 * 8
    result = sum(values[at : at + 8, :] for at in range(0, whole, 8))
    if whole < values.shape[0]:
        rest = values[whole:, :]
        result = result + jnp.concatenate([rest, jnp.zeros((8 - rest.shape[0], rest.shape[1]), rest.dtype)], axis=0)
    return result


def bias_sums(halves, count):
    shape = (ROUND, ROUND * count // 2)
    pick = jnp.where(
        remainder(lax.broadcasted_iota(jnp.int32, shape, 1), ROUND) == lax.broadcasted_iota(jnp.int32, shape, 0), 1.0, 0.0
    ).astype(jnp.bfloat16)
    return nn(pick, halves[0]) + nn(pick, halves[1])


def lifted(lift, part, halves, count):
    half = ROUND * count // 2
    return nn(lift[part, :, :half], halves[0]) + nn(lift[part, :, half:], halves[1])


def backward_kernel(bits, rows, tall_rows, pieces, clock,
                    a_all, b_all, c_all, mod, bias_rows, down_sums, key_mask, row_mask, lift, mod_low, frames, cot_in, query_in, key_in, value_in,
                    total_in, branch_in, midway_in, slope_in, active_in, change_in, turned_in, down_in,
                    block_out, frames_out, spread_out, a_out, b_out, c_out, ordered, norm_out,
                    weight, slabs, other_up, other_low, active, slope, query, key, value, x_ref, cot, change, d_attended,
                    midway, branch, down_acc, d_norm, d_midway, turned, totals, first_grads, second_grads, third_grads, recv, total,
                    quad_block, dmod, bias_out, spread, squares, table, answers,
                    weight_sem, stream_sem, load_sem, save_sem, send_sem, recv_sem, pair_send, pair_recv,
                    quad_send, quad_recv, quad_own, spread_send, spread_recv, spread_own,
                    answer_send, answer_recv):
    count = 1 << bits
    spots = Spots(bits)
    core = spots.core
    sibling = spots.device[CORE]
    tokens, width = x_ref.shape
    size = width // HEADS
    scale = size ** (-0.5)
    low, wide = jnp.bfloat16, jnp.float32
    span = 2 * tall_rows
    finals = []

    grads_load = local(down_in, first_grads, load_sem.at[0])
    order = [(c_all, s, True) for s in range(4)] + [(b_all, s, False) for s in range(4)]
    order += [(a_all, 3, False), (a_all, 0, False), (a_all, 1, False), (a_all, 2, False)]
    weights = {}

    def load_weight(index):
        if index < len(order):
            source, s, flat = order[index]
            part = source.at[pl.ds(s * width, width)] if flat else source.at[s]
            weights[index] = local(part, weight.at[index % 2], weight_sem.at[index % 2])

    streams = {}

    def load_stream(s):
        if s < 4:
            where = pl.ds(s * width, width)
            streams[s] = (
                local(slope_in.at[:, where], slope.at[s % 2], stream_sem.at[0, s % 2]),
                local(active_in.at[:, where], active.at[s % 2], stream_sem.at[1, s % 2]),
            )

    change_load = local(change_in, change, load_sem.at[1])
    load_weight(0)
    load_stream(0)
    load_weight(1)
    load_stream(1)
    loads = {
        name: local(source, target, load_sem.at[2 + index])
        for index, (name, source, target) in enumerate(
            (
                ("second", turned_in.at[2], turned.at[2]), ("midway", midway_in, midway), ("cot", cot_in, cot),
                ("branch", branch_in, branch), ("value", value_in, value), ("query", query_in, query), ("key", key_in, key),
                ("totals", total_in, totals), ("first", turned_in.at[0], turned.at[0]),
                ("attended", turned_in.at[1], turned.at[1]), ("x", frames, x_ref),
            )
        )
    }
    spots.greet()
    dmod[...] = jnp.zeros_like(dmod)
    bias_out[...] = jnp.zeros_like(bias_out)
    squares[...] = jnp.zeros_like(squares)

    grads = (third_grads, second_grads, first_grads)
    sums_at = (0, 1, 0)
    block_stage, frames_stage = change, d_attended
    down_copies = []

    def own(piece, member):
        kind, start, length, late = pieces[piece]
        index = spots.block(late, member)
        row = remainder(index, 2) * (tall_rows if kind == 2 else width)
        row = row + quotient(index, 4) * (span if kind == 2 else 4 * rows)
        return grads[kind].at[aligned(row + start, length)]

    def landed(piece, member):
        kind, start, length, _ = pieces[piece]
        return recv.at[kind, member - 1, pl.ds(start, length)]

    sent = {kind: [] for kind in range(3)}

    def pass_on(piece, member):
        kind, _, _, late = pieces[piece]
        place = top_place(member)
        sent[kind].append(
            remote(
                own(piece, member), landed(piece, member), send_sem.at[piece, member], recv_sem.at[piece, member],
                spots.partner(late, place),
            )
        )

    def summed(piece, member, body):
        parts = [member | 1 << place for place in range(top_place(member) + 1, bits - 1)]
        for part in parts:
            await_bytes(landed(piece, part), recv_sem.at[piece, part])
        kind, start, length, _ = pieces[piece]
        mine = own(piece, member)

        def strip(s):
            where = aligned(s * ROUND, ROUND)
            value = mine[where, :].astype(wide)
            for part in parts:
                value = value + recv[kind, part - 1, aligned(start + s * ROUND, ROUND), :].astype(wide)
            body(mine, where, s, value)

        repeat(length // ROUND, strip)

    def relay(piece, member):
        def body(mine, where, s, value):
            mine[where, :] = value.astype(low)

        summed(piece, member, body)
        pass_on(piece, member)

    left = {kind: len([1 for entry in pieces if entry[0] == kind]) for kind in range(3)}

    def settle(piece):
        kind, start, length, _ = pieces[piece]

        def body(mine, where, s, value):
            total[sums_at[kind], aligned(start + s * ROUND, ROUND), :] = value
            squares[...] = squares[...] + value * value

        if kind == 0:
            while down_copies:
                down_copies.pop().wait()
        summed(piece, 0, body)
        left[kind] -= 1
        if left[kind]:
            return
        if kind == 2:
            down_copies.append(local(total.at[0], c_out, save_sem.at[0]))
            return
        for lane in range(0, width, 128):
            for q in range(4):
                part = total[sums_at[kind], q * rows : (q + 1) * rows, lane : lane + 128]
                quad_block[kind, q, :, lane : lane + 128] = part.astype(low)
        out = (a_out, b_out)[kind]
        finals.append(local(quad_block.at[kind, spots.quad], out.at[spots.quad], quad_own.at[kind]).wait)
        for other in (1, 2, 3):
            device, spot = spots.near(other)
            copy = remote(
                quad_block.at[kind, spot], out.at[spots.quad], quad_send.at[kind, other], quad_recv.at[kind, other], device
            )
            finals.append(copy.wait)

    agenda = Agenda()

    def open_kind(kind):
        half = count // 2
        for member in range(half - 1, half // 2 - 1, -1):
            for piece, entry in enumerate(pieces):
                if entry[0] == kind:
                    pass_on(piece, member)
        begin, pace = clock["open"][kind]
        for piece, entry in enumerate(pieces):
            if entry[0] == kind:
                for at, member in enumerate(range(half // 2 - 1, 0, -1)):
                    agenda.service(agenda.now + begin + pace * at, functools.partial(relay, piece, member))
                agenda.service(agenda.now + begin + pace * (half // 2 - 1), functools.partial(settle, piece))

    def open_down():
        grads_load.wait()
        open_kind(2)

    pairs = {}

    def trade(index, source, target):
        pairs[index] = remote(source, target, pair_send.at[index], pair_recv.at[index], sibling)

    def over_strips(body):
        repeat(tokens // STRIP, lambda s: body(aligned(s * STRIP, STRIP, STRIP)))

    def over_tiles(body):
        repeat(width // TILE, lambda t: body(aligned(t * TILE, TILE, 128)))

    def add_row(ref, row, where, values):
        ref[row : row + 1, where] = ref[row : row + 1, where] + jnp.sum(values, axis=0, keepdims=True)

    everything = slice(None)

    def down_slice(s):
        slot = s % 2
        if s == 0:
            change_load.wait()
        weights[s].wait()
        for copy in streams[s]:
            copy.wait()

        def body(where):
            d_up = (nt(change[...], weight[slot, where, :]) * slope[slot, :, where]).astype(low)
            slabs[s, :, where] = d_up
            add_row(bias_out, 3 + s, where, d_up.astype(wide))
            part = nn(active[slot], weight[slot, :, where])
            down_acc[:, where] = part if s == 0 else down_acc[:, where] + part

        over_tiles(body)
        load_weight(s + 2)
        load_stream(s + 2)

    def trade_up():
        for t in range(2):
            trade(t, slabs.at[2 * (1 - core) + t], other_up.at[t])

    def up_gradient(t):
        if t == 0:
            loads["second"].wait()
        pairs[t].wait_recv()

        def body(where):
            def strip(m):
                down = aligned(m * 288, 288)
                result = nn(turned[2, 0, down, :], slabs[2 * core + t, :, where])
                result = result + nn(turned[2, 1, down, :], other_up[t, :, where])
                second_grads[aligned(t * width + m * 288, 288), where] = result.astype(low)

            repeat(width // 288, strip)

        over_tiles(body)

    def norm_two_slice(s):
        weights[4 + s].wait()

        def body(where):
            part = nt(slabs[s], weight[s % 2, where, :])
            d_norm[:, where] = part if s == 0 else d_norm[:, where] + part

        over_tiles(body)
        load_weight(6 + s)

    def upstream_of(where):
        return cot[where, :].astype(wide) * row_mask[where, :]

    def norm_back(values, gradient, gain):
        unit, root = normalized(values)
        spread = gain * gradient
        back = root * (
            spread
            - jnp.mean(spread, axis=-1, keepdims=True)
            - unit * jnp.mean(spread * unit, axis=-1, keepdims=True)
        )
        return unit, back

    def back_second():
        for name in ("midway", "cot", "branch"):
            loads[name].wait()
        for t in range(2):
            pairs[t].wait_send()

        def body(where):
            gradient = d_norm[where, :]
            unit, back = norm_back(midway[where, :], gradient, 1.0 + mod[4:5, :])
            middle = upstream_of(where) + back
            d_midway[where, :] = middle
            d_branch = (mod[2:3, :] * middle).astype(low)
            slabs[3, where, :] = d_branch
            add_row(dmod, 3, everything, gradient)
            add_row(dmod, 4, everything, gradient * unit)
            add_row(dmod, 2, everything, middle * branch[where, :])
            add_row(bias_out, 2, everything, d_branch.astype(wide))

        over_strips(body)

    def back_attended():
        weights[8].wait()

        def body(where):
            d_attended[:, where] = nt(slabs[3], weight[0, where, :]).astype(low)

        over_tiles(body)
        load_weight(10)
        for name in ("value", "query", "key", "totals"):
            loads[name].wait()
        slope[...] = jnp.zeros_like(slope)
        branch[...] = jnp.zeros_like(branch)

    def attend_back(head):
        start, reach, offset = head_window(head, size)
        where = slice(start, start + reach)
        chosen = only_head(query[:, where], offset, size)
        scores = nt(chosen, key[:, where])
        scores = jnp.where(key_mask[0:1, :] > 0, scores * scale, MASK_VALUE)
        soft = jnp.exp(scores - totals[:, head : head + 1])
        given = only_head(d_attended[:, where], offset, size)
        d_soft = nt(given, value[:, where])
        d_scores = (soft * (d_soft - jnp.sum(soft * d_soft, axis=-1, keepdims=True))).astype(low)
        slope[0, :, where] = slope[0, :, where] + nn(d_scores, only_head(key[:, where], offset, size))
        slope[1, :, where] = slope[1, :, where] + tn(d_scores, chosen)
        branch[:, where] = branch[:, where] + tn(soft.astype(low), given)

    def leave_attention():
        slabs[0] = (slope[0] * scale).astype(low)
        slabs[1] = (slope[1] * scale).astype(low)
        slabs[2] = branch[...].astype(low)
        for t in range(2):
            trade(2 + t, slabs.at[2 * (1 - core) + t], other_low.at[t])
        bias_out[0:1, :] = jnp.sum(slabs[0].astype(wide), axis=0, keepdims=True)
        bias_out[1:2, :] = jnp.sum(slabs[2].astype(wide), axis=0, keepdims=True)

    def leave_block():
        def body(where):
            down = down_acc[where, :] + bias_rows[7:8, :]
            add_row(dmod, 5, everything, upstream_of(where) * down)
            block_stage[where, :] = ((midway[where, :] + mod[5:6, :] * down) * row_mask[where, :]).astype(low)

        over_strips(body)
        finals.append(local(block_stage, block_out, save_sem.at[1]).wait)

    def low_gradient(t):
        if t == 0:
            loads["first"].wait()
            loads["attended"].wait()
        pairs[2 + t].wait_recv()
        at = 2 * core + t
        which = quotient(at, 3)

        def body(where):
            def strip(m):
                down = aligned(m * 288, 288)
                result = nn(turned[which, 0, down, :], slabs[at, :, where])
                result = result + nn(turned[which, 1, down, :], other_low[t, :, where])
                third_grads[aligned(t * width + m * 288, 288), where] = result.astype(low)

            repeat(width // 288, strip)

        over_tiles(body)

    def norm_one_slice(s):
        weights[9 + s].wait()

        def body(where):
            part = nt(slabs[s], weight[(9 + s) % 2, where, :])
            d_norm[:, where] = part if s == 0 else d_norm[:, where] + part

        over_tiles(body)
        load_weight(11 + s)

    def back_first():
        loads["x"].wait()

        def body(where):
            gradient = d_norm[where, :]
            unit, back = norm_back(x_ref[where, :].astype(wide), gradient, 1.0 + mod[1:2, :])
            add_row(dmod, 0, everything, gradient)
            add_row(dmod, 1, everything, gradient * unit)
            frames_stage[where, :] = (back + d_midway[where, :]).astype(low)

        over_strips(body)
        finals.append(local(frames_stage, frames_out, save_sem.at[2]).wait)

    spread_copies = []

    def spread_step(step):
        if step == 0:
            spread_start.wait()
        else:
            spread_copies[step - 1].wait_recv()
        if step == bits:
            use_spread()
            return
        held = pl.ds(0, ROUND << step)
        copy = remote(
            spread_out.at[held], spread_out.at[pl.ds(ROUND << step, ROUND << step)], spread_send.at[step],
            spread_recv.at[step], spots.device[SPREAD(bits)[step]],
        )
        spread_copies.append(copy)
        finals.append(copy.wait_send)
        agenda.service(agenda.now + clock["spread"], functools.partial(spread_step, step + 1))

    def start_spread():
        nonlocal spread_start
        bias_out[7:8, :] = down_sums[0:1, :]
        spread[...] = jnp.concatenate([dmod[...], bias_out[...]], axis=0).astype(low)
        spread_start = local(spread, spread_out.at[pl.ds(0, ROUND)], spread_own)
        agenda.service(agenda.now + 1.0, functools.partial(spread_step, 0))

    def use_spread():
        half = ROUND * count // 2
        copies = [local(spread_out.at[pl.ds(t * half, half)], active.at[t], stream_sem.at[1, t]) for t in range(2)]
        for copy in copies:
            copy.wait()
        both = bias_sums(active, count)
        squares[...] = squares[...] + both * both * (1.0 / count)
        member = remainder(lax.broadcasted_iota(jnp.int32, (half, rows), 0), ROUND)
        partial = [jnp.zeros((half, rows), wide) for _ in range(2)]
        for part in range(6):
            where = slice(part * width, (part + 1) * width)
            value = lifted(lift, part, active, count)
            squares[0:8, :] = squares[0:8, :] + folded_rows(value * value)
            for t in range(2):
                partial[t] = partial[t] + jnp.where(member == part, nt(active[t], mod_low[:, where]), 0.0)
        table[...] = jnp.zeros_like(table)
        shape = (count // 2, half)
        gathers = jnp.where(
            quotient(lax.broadcasted_iota(jnp.int32, shape, 1), ROUND) == lax.broadcasted_iota(jnp.int32, shape, 0), 1.0, 0.0
        )
        for t in range(2):
            table[t * count // 2 : (t + 1) * count // 2, 0:rows] = jnp.dot(
                gathers, partial[t], preferred_element_type=wide, precision=lax.Precision.HIGHEST
            )

    def answer():
        total_square = jnp.sum(squares[...], axis=0, keepdims=True)
        folded = sum(total_square[:, at : at + 128] for at in range(0, width, 128))
        table[count : count + 8, :] = jnp.broadcast_to(folded, (8, 128))
        slot = lax.broadcasted_iota(jnp.int32, (count, 128), 0)
        for step, bit in enumerate(SPREAD(bits)):
            copy = remote(table, answers.at[step], answer_send.at[step], answer_recv.at[step], spots.device[bit])
            copy.wait()
            given = jnp.where(remainder(quotient(slot, 1 << step), 2) == 1, answers[step, 0:count, :], table[0:count, :])
            summed_up = table[count : count + 8, :] + answers[step, count : count + 8, :]
            table[0:count, :] = given
            table[count : count + 8, :] = summed_up
        for member in range(count):
            index = spots.me
            for step, bit in enumerate(SPREAD(bits)):
                if member >> step & 1:
                    index = index + spots.delta[bit]
            ordered[pl.ds(index, 1), :] = table[member : member + 1, :]
        norm_out[...] = jnp.broadcast_to(jnp.sqrt(jnp.sum(table[count : count + 8, :], axis=1, keepdims=True)), (8, 128))

    spread_start = None
    takes = clock["takes"]
    agenda.step(2.0, open_down)
    for s in range(4):
        agenda.step(takes["down"], functools.partial(down_slice, s))
    agenda.step(0.3, trade_up)
    for t in range(2):
        agenda.step(takes["gradient"], functools.partial(up_gradient, t))
    agenda.step(0.5, lambda: open_kind(1))
    for s in range(4):
        agenda.step(takes["matmul"], functools.partial(norm_two_slice, s))
    agenda.step(takes["norm"], back_second)
    agenda.step(takes["matmul"], back_attended)
    for head in range(HEADS):
        agenda.step(takes["head"], functools.partial(attend_back, head))
    agenda.step(1.0, leave_attention)
    agenda.step(takes["norm"], leave_block)
    for t in range(2):
        agenda.step(takes["gradient"], functools.partial(low_gradient, t))
    agenda.step(0.5, lambda: open_kind(0))
    for s in range(3):
        agenda.step(takes["matmul"], functools.partial(norm_one_slice, s))
    agenda.step(takes["norm"], back_first)
    agenda.step(0.5, start_spread)
    agenda.emit()
    answer()
    for kind in range(3):
        for copy in sent[kind]:
            copy.wait_send()
    for t in range(2):
        pairs[2 + t].wait_send()
    for done in finals:
        done()


BACK_CLOCK = {
    "spread": 4.0,
    "open": ((22.0, 4.0), (24.0, 5.5), (20.0, 5.0)),
    "takes": {"down": 4.2, "gradient": 4.2, "matmul": 2.1, "norm": 1.7, "head": 0.42},
}


def backward(weights, mod, bias_rows, down_sums, key_mask, row_mask, lift, mod_low, frames, cot, saved, rows, bits, pieces=PIECES, clock=BACK_CLOCK):
    a_all, b_all, c_all = weights
    width = a_all.shape[-1]
    count = 1 << bits
    hidden = c_all.shape[0]
    tall = hidden // count
    tokens = frames.shape[0]
    low, wide = jnp.bfloat16, jnp.float32

    def shaped(*sizes, dtype=low):
        return jax.ShapeDtypeStruct(sizes, dtype)

    anywhere = pl.BlockSpec(memory_space=pl.ANY)
    near = pl.BlockSpec(memory_space=pltpu.VMEM)
    dma = pltpu.SemaphoreType.DMA
    v = pltpu.VMEM
    kinds = len(pieces)
    scratch = [
        v((2, width, width), low), v((4, tokens, width), low),
        v((2, tokens, width), low), v((2, tokens, width), low),
        v((2, tokens, width), low), v((2, tokens, width), wide),
        v((tokens, width), low), v((tokens, width), low), v((tokens, width), low),
        v((tokens, width), low), v((tokens, width), low), v((tokens, width), low), v((tokens, width), low),
        v((tokens, width), wide), v((tokens, width), wide),
        v((tokens, width), wide), v((tokens, width), wide), v((tokens, width), wide),
        v((3, 2, width, tokens), low), v((tokens, 128), wide),
        v((2 * width, width), low), v((2 * width, width), low), v((2 * width, width), low),
        v((3, count // 2 - 1, 4 * rows, width), low), v((2, 4 * rows, width), wide), v((2, 4, rows, width), low),
        v((8, width), wide), v((8, width), wide), v((ROUND, width), low),
        v((ROUND, width), wide), v((count + 8, 128), wide), v((bits, count + 8, 128), wide),
        dma((2,)), dma((2, 2)), dma((13,)), dma((3,)), dma((kinds, count // 2)), dma((kinds, count // 2)),
        dma((4,)), dma((4,)), dma((2, 4)), dma((2, 4)), dma((2,)), dma((bits,)), dma((bits,)), dma, dma((bits,)), dma((bits,)),
    ]
    share = shaped(4, rows, width)
    return pl.pallas_call(
        functools.partial(backward_kernel, bits, rows, tall, pieces, clock),
        out_shape=(
            shaped(tokens, width), shaped(tokens, width), shaped(ROUND * count, width),
            share, share, shaped(tall, width, dtype=wide), shaped(count, 128, dtype=wide), shaped(8, 128, dtype=wide),
        ),
        in_specs=[anywhere] * 3 + [near] * 7 + [anywhere] * (2 + len(saved)),
        out_specs=[anywhere] * 6 + [near] * 2,
        scratch_shapes=scratch,
        compiler_params=pltpu.CompilerParams(collective_id=1, has_side_effects=True, vmem_limit_bytes=63 * 1024 * 1024),
        cost_estimate=pl.CostEstimate(flops=18_000_000_000, bytes_accessed=400_000_000, transcendentals=3_000_000),
        name="backward_reduce",
    )(a_all, b_all, c_all, mod, bias_rows, down_sums, key_mask, row_mask, lift, mod_low, frames, cot, *saved)


def update_kernel(count, a_in, b_in, c_in, spread_in, lift, norm, bias, bias_state, *rest):
    masters, states, rest = rest[:5], rest[5:10], rest[10:]
    grads, news, news_state, rest = rest[:5], rest[5:10], rest[10:15], rest[15:]
    (bias_grad, bias_new, bias_state_new), rest = rest[:3], rest[3:]
    w, st, g, rest = rest[:5], rest[5:10], rest[10:15], rest[15:]
    a_sum, b_sum, spread, sums, in_sem, load_sem, out_sem = rest
    wide = jnp.float32
    width = a_sum.shape[2]
    half = ROUND * count // 2
    inputs = [
        local(source, target, in_sem.at[index])
        for index, (source, target) in enumerate(
            (
                (spread_in.at[pl.ds(0, half)], spread.at[0]), (spread_in.at[pl.ds(half, half)], spread.at[1]),
                (a_in, a_sum), (b_in, b_sum), (c_in, g[4]),
            )
        )
    ]
    sequence = (0, 3, 4, 1, 2)
    loads = {
        k: (local(masters[k], w[k], load_sem.at[0, k]), local(states[k], st[k], load_sem.at[1, k])) for k in sequence
    }
    factor = jnp.minimum(1.0, CLIP / (norm[0:1, 0:1] + 1e-06))
    for copy in inputs:
        copy.wait()
    both = bias_sums(spread, count)
    sums[...] = jnp.zeros_like(sums)
    sums[0:6, :] = both[0:6, :]
    sums[6:14, :] = both[8:16, :]

    def adam(weight, first_moment, second_moment, average, raw):
        grad = raw * factor
        moved = FIRST_DECAY * first_moment + (1.0 - FIRST_DECAY) * grad
        around = SECOND_DECAY * second_moment + (1.0 - SECOND_DECAY) * grad * grad
        step = (moved / (1.0 - FIRST_DECAY**STEPS)) / (jnp.sqrt(around / (1.0 - SECOND_DECAY**STEPS)) + ADAM_EPS)
        fresh = weight - RATE * (step + WEIGHT_DECAY * weight)
        return grad, fresh, moved, around, AVERAGE_DECAY * average + (1.0 - AVERAGE_DECAY) * fresh

    share = bias.shape[1]
    first = (lax.axis_index("wide") * 2 + lax.axis_index("narrow")) * share
    top = quotient(first, width)
    pair = jnp.concatenate([sums[pl.ds(top, 1), :], sums[pl.ds(top + 1, 1), :]], axis=1)
    pair = jnp.broadcast_to(pair, (8, 2 * width))
    bias_raw = pltpu.roll(pair, 2 * width - (first - top * width), 1)[0:1, :share]
    results = adam(bias[...], bias_state[0:1, :], bias_state[1:2, :], bias_state[2:3, :], bias_raw)
    bias_grad[...], bias_new[...] = results[:2]
    for part in range(3):
        bias_state_new[part : part + 1, :] = results[2 + part]
    stores = []
    for k in sequence:
        for copy in loads[k]:
            copy.wait()
        tile = 128 if k == 4 else TILE
        for part in range(w[k].shape[1] // width):

            def body(t, k=k, tile=tile, part=part):
                inner = aligned(t * tile, tile, 128)
                where = aligned(part * width + t * tile, tile, 128)
                if k == 0:
                    raw = nn(lift[part, :, :half], spread[0, :, inner]) + nn(lift[part, :, half:], spread[1, :, inner])
                elif k == 4:
                    raw = g[4][:, where]
                else:
                    raw = (b_sum if k == 3 else a_sum)[3 if k == 2 else part, :, inner].astype(wide)
                results = adam(w[k][:, where], st[k][0, :, where], st[k][1, :, where], st[k][2, :, where], raw)
                g[k][:, where], w[k][:, where] = results[:2]
                for slot in range(3):
                    st[k][slot, :, where] = results[2 + slot]

            repeat(width // tile, body)
        for at, (source, target) in enumerate(((g[k], grads[k]), (w[k], news[k]), (st[k], news_state[k]))):
            stores.append(local(source, target, out_sem.at[at, k]))
    for copy in stores:
        copy.wait()


def update(sums, spread, lift, norm, masters, states):
    a_sum, b_sum, c_sum = sums
    count = spread.shape[0] // ROUND
    wide = jnp.float32
    anywhere = pl.BlockSpec(memory_space=pl.ANY)
    near = pl.BlockSpec(memory_space=pltpu.VMEM)
    dma = pltpu.SemaphoreType.DMA

    def like(member):
        return jax.ShapeDtypeStruct(member.shape, member.dtype)

    width = a_sum.shape[2]
    bias, bias_state = masters[5].reshape(1, -1), states[5]
    outs = [like(member) for member in masters[:5]] * 2 + [like(member) for member in states[:5]]
    outs += [like(bias), like(bias), like(bias_state)]
    buffers = [pltpu.VMEM(member.shape, wide) for member in tuple(masters[:5]) + tuple(states[:5]) + tuple(masters[:5])]
    results = pl.pallas_call(
        functools.partial(update_kernel, count),
        out_shape=tuple(outs),
        in_specs=[anywhere] * 4 + [near] * 4 + [anywhere] * 10,
        out_specs=tuple([anywhere] * 15 + [near] * 3),
        scratch_shapes=buffers + [
            pltpu.VMEM(a_sum.shape, a_sum.dtype), pltpu.VMEM(b_sum.shape, b_sum.dtype),
            pltpu.VMEM((2, spread.shape[0] // 2, width), spread.dtype), pltpu.VMEM((ROUND, width), wide),
            dma((5,)), dma((2, 5)), dma((3, 5)),
        ],
        compiler_params=pltpu.CompilerParams(vmem_limit_bytes=56 * 1024 * 1024),
        cost_estimate=pl.CostEstimate(flops=100_000_000, bytes_accessed=40_000_000, transcendentals=1_000_000),
        name="update",
    )(a_sum, b_sum, c_sum, spread, lift, norm, bias, bias_state, *masters[:5], *states[:5])
    grads, news, news_state = results[:5], results[5:10], results[10:15]
    bias_grad, bias_new, bias_state_new = results[15:]
    grads = tuple(grads) + (bias_grad.reshape(-1),)
    news = tuple(news) + (bias_new.reshape(-1),)
    return grads, news, tuple(news_state) + (bias_state_new,)


def masks(order, member):
    return sum(1 << bit for place, bit in enumerate(order) if member >> place & 1)


def me_index():
    return lax.axis_index("wide") * 2 + lax.axis_index("narrow")


def device(index):
    return (index // 2, lax.rem(index, 2))


def own_plane(me):
    return lax.rem(me // 2, 2)


def flip(index, mask):
    out = index
    bit = 0
    while mask >> bit:
        if mask >> bit & 1:
            value = lax.rem(out // (1 << bit), 2)
            out = out + (1 << bit) * (1 - 2 * value)
        bit += 1
    return out


def block_of(me, pair, member, bits):
    plane = own_plane(me)
    last = 1 << (bits - 1)
    if member & last:
        rest = member - last
        zero = flip(flip(me, 1 << CORE), masks(pair[1], rest))
        one = flip(flip(me, 1 << CORE), masks(pair[0], rest))
    else:
        zero = flip(me, masks(pair[0], member))
        one = flip(me, masks(pair[1], member))
    return jnp.where(plane == 0, zero, one)


def partner_of(me, pair, place):
    zero = flip(me, 1 << pair[0][place])
    if pair[0][place] == pair[1][place]:
        return zero
    return jnp.where(own_plane(me) == 0, zero, flip(me, 1 << pair[1][place]))


def greet(me, bits):
    barrier = pltpu.get_barrier_semaphore()
    partners = [flip(me, 1 << bit) for bit in range(bits)] + [flip(me, 3)]
    for partner in partners:
        pl.semaphore_signal(barrier, inc=1, device_id=device(partner), device_id_type=MESH)
    pl.semaphore_wait(barrier, len(partners))


def gather_kernel(bits, rows, lates, a_src, b_src, c_src, a_out, b_out, c_out,
                  stage, block, c_block, quad_send, quad_recv, own_sem, keep_sem, send_sem, recv_sem):
    count = 1 << bits
    me = me_index()
    quad, spot = lax.rem(me, 4), me // 4
    pairs = [orders(bits, late) for late in lates]
    outs = (a_out, b_out, c_out)

    def place(kind, index):
        q, j = lax.rem(index, 4), index // 4
        return outs[kind].at[q, j] if kind < 2 else outs[kind].at[j, q]

    def send(kind, member, step, source):
        target = member | 1 << step
        return pltpu.make_async_remote_copy(
            src_ref=source,
            dst_ref=place(kind, block_of(me, pairs[kind], member, bits)),
            send_sem=send_sem.at[kind, target],
            recv_sem=recv_sem.at[kind, target],
            device_id=device(partner_of(me, pairs[kind], step)),
            device_id_type=MESH,
        )

    own = []
    for kind, source in enumerate((a_src, b_src)):
        own.append(pltpu.make_async_copy(source.at[quad], stage.at[kind, quad], own_sem.at[kind]))
    own.append(pltpu.make_async_copy(c_src, c_block, own_sem.at[2]))
    for copy in own:
        copy.start()
    greet(me, bits)
    quads = []
    for kind, source in enumerate((a_src, b_src)):
        for other in (1, 2, 3):
            copy = pltpu.make_async_remote_copy(
                src_ref=source.at[flip(quad, other)],
                dst_ref=stage.at[kind, quad],
                send_sem=quad_send.at[kind, other],
                recv_sem=quad_recv.at[kind, other],
                device_id=device(flip(me, other)),
                device_id_type=MESH,
            )
            copy.start()
            quads.append(copy)
    sends = []
    keeps = []

    def launch(kind, member, source):
        for step in range(top_place(member) + 1, bits):
            copy = send(kind, member, step, source)
            copy.start()
            sends.append(copy)

    def keep(kind, source):
        copy = pltpu.make_async_copy(source, place(kind, me), keep_sem.at[kind])
        copy.start()
        keeps.append(copy)

    own[2].wait()
    launch(2, 0, c_block)
    keep(2, c_block)
    padded = block.shape[1]
    for kind in (0, 1):
        own[kind].wait()
        for copy in quads[3 * kind:3 * kind + 3]:
            copy.wait_recv()
        for lane in range(0, stage.shape[3], 128):
            parts = [stage[kind, q, :, lane:lane + 128].astype(jnp.float32) for q in range(4)]
            if padded > 4 * rows:
                parts.append(jnp.zeros((padded - 4 * rows, 128), jnp.float32))
            block[kind, :, lane:lane + 128] = jnp.concatenate(parts, axis=0).astype(jnp.bfloat16)
        launch(kind, 0, block.at[kind])
        keep(kind, block.at[kind])

    def arrived(kind, member):
        spot_ref = place(kind, block_of(me, pairs[kind], member, bits))
        pltpu.make_async_copy(spot_ref, spot_ref, recv_sem.at[kind, member]).wait()
        return spot_ref

    for member in range(1, count):
        for kind in (2, 0, 1):
            launch(kind, member, arrived(kind, member))
    for copy in sends + quads:
        copy.wait_send()
    for copy in keeps:
        copy.wait()


def gather(a_src, b_src, c_src, count, lates=(False, False, False)):
    bits = count.bit_length() - 1
    rows, columns = a_src.shape[1:]
    padded = -(-4 * rows // 16) * 16
    c_padded = -(-c_src.shape[0] // 16) * 16
    if c_padded != c_src.shape[0]:
        c_src = jnp.pad(c_src, ((0, c_padded - c_src.shape[0]), (0, 0)))
    kinds = 3
    anywhere = pl.BlockSpec(memory_space=pl.ANY)
    big = jax.ShapeDtypeStruct((4, count // 4, padded, columns), jnp.bfloat16)
    tall = jax.ShapeDtypeStruct((count // 4, 4, c_padded, columns), jnp.bfloat16)
    a_all, b_all, c_all = pl.pallas_call(
        functools.partial(gather_kernel, bits, rows, lates),
        out_shape=(big, big, tall),
        in_specs=[anywhere] * 3,
        out_specs=(anywhere,) * 3,
        scratch_shapes=[
            pltpu.VMEM((2, 4, rows, columns), jnp.bfloat16),
            pltpu.VMEM((2, padded, columns), jnp.bfloat16),
            pltpu.VMEM((c_padded, columns), jnp.bfloat16),
            pltpu.SemaphoreType.DMA((2, 4)),
            pltpu.SemaphoreType.DMA((2, 4)),
            pltpu.SemaphoreType.DMA((3,)),
            pltpu.SemaphoreType.DMA((3,)),
            pltpu.SemaphoreType.DMA((kinds, count)),
            pltpu.SemaphoreType.DMA((kinds, count)),
        ],
        compiler_params=pltpu.CompilerParams(collective_id=2, has_side_effects=True),
        cost_estimate=pl.CostEstimate(flops=0, bytes_accessed=400_000_000, transcendentals=0),
        name="gather_weights",
    )(a_src, b_src, c_src)
    return a_all, b_all, c_all


def reduce_kernel(bits, rows, lates, a_in, b_in, c_in, a_out, b_out, c_out,
                  own, recv, quad_block, total, own_sem, send_sem, recv_sem, quad_send, quad_recv, quad_own, total_sem):
    count = 1 << bits
    half = count // 2
    me = me_index()
    quad = lax.rem(me, 4)
    pairs = [orders(bits, late) for late in lates]
    ins = (a_in, b_in, c_in)
    kinds = (2, 1, 0)

    def place(kind, index):
        q, j = lax.rem(index, 4), index // 4
        return ins[kind].at[q, j] if kind < 2 else ins[kind].at[j, q]

    loads = {}
    for member in range(half - 1, -1, -1):
        for kind in kinds:
            loads[kind, member] = pltpu.make_async_copy(
                place(kind, block_of(me, pairs[kind], member, bits)), own.at[kind, member], own_sem.at[kind, member]
            )
    sends = []

    def send(kind, member, source):
        step = top_place(member)
        copy = pltpu.make_async_remote_copy(
            src_ref=source,
            dst_ref=recv.at[kind, member],
            send_sem=send_sem.at[kind, member],
            recv_sem=recv_sem.at[kind, member],
            device_id=device(partner_of(me, pairs[kind], step)),
            device_id_type=MESH,
        )
        copy.start()
        sends.append(copy)

    for kind in kinds:
        loads[kind, half - 1].start()
    greet(me, bits)
    for member in range(half - 1, -1, -1):
        for kind in kinds:
            send(kind, member + half, place(kind, block_of(me, pairs[kind], member + half, bits)))
            if member < half - 1:
                loads[kind, member].start()

    padded, columns = own.shape[2:]

    def ready(kind, member):
        loads[kind, member].wait()
        parts = [member | 1 << step for step in range(top_place(member) + 1, bits)]
        for part in parts:
            pltpu.make_async_copy(recv.at[kind, part], recv.at[kind, part], recv_sem.at[kind, part]).wait()
        return parts

    def summed(kind, member, parts, where):
        value = own[kind, member, where, :].astype(jnp.float32)
        for part in parts:
            value = value + recv[kind, part, where, :].astype(jnp.float32)
        return value

    for member in range(half - 1, 0, -1):
        for kind in kinds:
            parts = ready(kind, member)

            def strip(s, carry, kind=kind, member=member, parts=parts):
                where = pl.ds(pl.multiple_of(s * 16, 16), 16)
                own[kind, member, where, :] = summed(kind, member, parts, where).astype(jnp.bfloat16)
                return carry

            lax.fori_loop(0, padded // 16, strip, 0)
            send(kind, member, own.at[kind, member])

    copies = []
    for kind in kinds:
        parts = ready(kind, 0)

        def strip(s, carry, kind=kind, parts=parts):
            where = pl.ds(pl.multiple_of(s * 16, 16), 16)
            total[kind, where, :] = summed(kind, 0, parts, where)
            return carry

        lax.fori_loop(0, padded // 16, strip, 0)
        if kind == 2:
            copy = pltpu.make_async_copy(total.at[2], c_out, total_sem)
            copy.start()
            copies.append(copy)
            continue
        out = (a_out, b_out)[kind]
        for lane in range(0, columns, 128):
            for q in range(4):
                quad_block[kind, q, :, lane:lane + 128] = total[kind, q * rows:(q + 1) * rows, lane:lane + 128].astype(jnp.bfloat16)
        copy = pltpu.make_async_copy(quad_block.at[kind, quad], out.at[quad], quad_own.at[kind])
        copy.start()
        copies.append(copy)
        for other in (1, 2, 3):
            copy = pltpu.make_async_remote_copy(
                src_ref=quad_block.at[kind, flip(quad, other)],
                dst_ref=out.at[quad],
                send_sem=quad_send.at[kind, other],
                recv_sem=quad_recv.at[kind, other],
                device_id=device(flip(me, other)),
                device_id_type=MESH,
            )
            copy.start()
            copies.append(copy)
    for copy in copies:
        copy.wait()
    for copy in sends:
        copy.wait_send()


def reduce(a_in, b_in, c_in, rows, lates=(False, False, False)):
    count = a_in.shape[1] * 4
    bits = count.bit_length() - 1
    padded, columns = a_in.shape[2:]
    anywhere = pl.BlockSpec(memory_space=pl.ANY)
    share = jax.ShapeDtypeStruct((4, rows, columns), jnp.bfloat16)
    return pl.pallas_call(
        functools.partial(reduce_kernel, bits, rows, lates),
        out_shape=(share, share, jax.ShapeDtypeStruct((padded, columns), jnp.float32)),
        in_specs=[anywhere] * 3,
        out_specs=(anywhere,) * 3,
        scratch_shapes=[
            pltpu.VMEM((3, count // 2, padded, columns), jnp.bfloat16),
            pltpu.VMEM((3, count, padded, columns), jnp.bfloat16),
            pltpu.VMEM((2, 4, rows, columns), jnp.bfloat16),
            pltpu.VMEM((3, padded, columns), jnp.float32),
            pltpu.SemaphoreType.DMA((3, count // 2)),
            pltpu.SemaphoreType.DMA((3, count)),
            pltpu.SemaphoreType.DMA((3, count)),
            pltpu.SemaphoreType.DMA((2, 4)),
            pltpu.SemaphoreType.DMA((2, 4)),
            pltpu.SemaphoreType.DMA((2,)),
            pltpu.SemaphoreType.DMA,
        ],
        compiler_params=pltpu.CompilerParams(collective_id=3, has_side_effects=True, vmem_limit_bytes=62 * 1024 * 1024),
        cost_estimate=pl.CostEstimate(flops=0, bytes_accessed=400_000_000, transcendentals=0),
        name="reduce_gradients",
    )(a_in, b_in, c_in)


def layer_norm(values):
    centre = jnp.mean(values, axis=-1, keepdims=True)
    centred = values - centre
    spread = jnp.mean(centred * centred, axis=-1, keepdims=True)
    return centred * lax.rsqrt(spread + NORM_EPS)


def modulate(values, shift_part, scale_part):
    return layer_norm(values) * (1.0 + scale_part) + shift_part


def silu_act(values):
    return values * jax.nn.sigmoid(values)


def gelu_tanh(values):
    inner = 0.7978845608028654 * (values + 0.044715 * values * values * values)
    return 0.5 * values * (1.0 + jnp.tanh(inner))


def slot_mask(grid, frame_len):
    area = grid[:, 0] * grid[:, 1]
    return lax.broadcasted_iota(jnp.int32, (grid.shape[0], frame_len), 1) < area[:, None]


def split_biases(biases, model_width, hidden_width):
    edges = [
        6 * model_width,
        7 * model_width,
        8 * model_width,
        9 * model_width,
        9 * model_width + hidden_width,
    ]
    return jnp.split(biases, edges)


def adam_update(weight, state, grad):
    first = FIRST_DECAY * state[0] + (1.0 - FIRST_DECAY) * grad
    second = SECOND_DECAY * state[1] + (1.0 - SECOND_DECAY) * grad * grad
    first_hat = first / (1.0 - FIRST_DECAY**STEPS)
    second_hat = second / (1.0 - SECOND_DECAY**STEPS)
    new_weight = weight - RATE * (
        first_hat / (jnp.sqrt(second_hat) + ADAM_EPS) + WEIGHT_DECAY * weight
    )
    average = AVERAGE_DECAY * state[2] + (1.0 - AVERAGE_DECAY) * new_weight
    return (new_weight, jnp.stack([first, second, average]))


def attention_scores(query_heads, key_heads, valid_slots, score_scale):
    scores = (
        jnp.einsum("fqhs,fkhs->fhqk", query_heads, key_heads, preferred_element_type=jnp.float32)
        * score_scale
    )
    return jnp.where(valid_slots[:, None, None, :], scores, MASK_VALUE)


def token_sum(values):
    return jnp.sum(values, axis=(0, 1), dtype=jnp.float32)


def exchange(packets):
    return lax.all_to_all(packets, AXES, split_axis=0, concat_axis=0, tiled=True)


def plain_shards(
    frames_in,
    conditioning,
    grid,
    cotangent,
    mod_weight,
    qkv_weight,
    out_weight,
    up_weight,
    down_weight,
    biases,
    mod_state,
    qkv_state,
    out_state,
    up_state,
    down_state,
    bias_state,
):
    frame_count, frame_len, model_width = frames_in.shape
    hidden_width = up_weight.shape[1]
    head_size = model_width // HEADS
    score_scale = head_size ** (-0.5)
    head_shape = (frame_count, frame_len, HEADS, head_size)
    count = lax.axis_size("wide") * lax.axis_size("narrow")
    rows = mod_weight.shape[0]
    tall_rows = down_weight.shape[0]
    low = jnp.bfloat16

    def slices(member):
        return member.reshape(rows, 4, model_width).transpose(1, 0, 2)

    a_src = slices(jnp.concatenate([qkv_weight.astype(low), out_weight.astype(low)], axis=1))
    b_src = slices(up_weight.astype(low))
    a_all, b_all, c_all = gather(a_src, b_src, down_weight.astype(low), count, (False, False, True))
    a_all = a_all[:, :, : 4 * rows].reshape(4, model_width, model_width)
    up_low = b_all[:, :, : 4 * rows].reshape(4, model_width, model_width)
    down_low = c_all[:, :, :tall_rows].reshape(hidden_width, model_width)
    query_low, key_low, value_low, out_low = (a_all[index] for index in range(4))

    cond_f = conditioning.astype(jnp.float32)
    silu_low = silu_act(cond_f).astype(low)
    mod_low = mod_weight.astype(low)
    first = exchange(
        jnp.concatenate(
            [
                silu_low.reshape(count, rows),
                jnp.broadcast_to(biases.astype(low)[None], (count, biases.shape[0])),
            ],
            axis=1,
        )
    )
    silu_rows = first[:, :rows]
    bias_low = first[:, rows:].reshape(-1)
    mod_terms = exchange(jnp.dot(silu_rows, mod_low, preferred_element_type=jnp.float32))
    mod_bias, query_bias, value_bias, out_bias, up_bias, down_bias = split_biases(
        bias_low.astype(jnp.float32), model_width, hidden_width
    )
    modulation = jnp.sum(mod_terms, axis=0, keepdims=True) + mod_bias
    valid_slots = slot_mask(grid, frame_len)
    row_mask = valid_slots[:, :, None].astype(jnp.float32)
    frames_f = frames_in.astype(jnp.float32)
    shift_attn, scale_attn, gate_attn, shift_mlp, scale_mlp, gate_mlp = jnp.split(
        modulation[:, None, :], 6, axis=-1
    )
    norm_one = modulate(frames_f, shift_attn, scale_attn).astype(low)

    def project(values, weight):
        return jnp.einsum("fbd,de->fbe", values, weight, preferred_element_type=jnp.float32)

    query_heads = (project(norm_one, query_low) + query_bias).astype(low).reshape(head_shape)
    key_heads = project(norm_one, key_low).astype(low).reshape(head_shape)
    value_heads = (project(norm_one, value_low) + value_bias).astype(low).reshape(head_shape)
    scores = attention_scores(query_heads, key_heads, valid_slots, score_scale)
    row_max = jnp.max(scores, axis=-1, keepdims=True)
    exponent = jnp.exp(scores - row_max)
    row_total = jnp.sum(exponent, axis=-1, keepdims=True)
    log_total = row_max + jnp.log(row_total)
    attention = (exponent / row_total).astype(low)
    attended = jnp.einsum(
        "fhqk,fkhs->fqhs", attention, value_heads, preferred_element_type=jnp.float32
    )
    attended = attended.reshape(frame_count, frame_len, model_width).astype(low)
    branch = project(attended, out_low) + out_bias
    midway = frames_f + gate_attn * branch
    norm_two = modulate(midway, shift_mlp, scale_mlp).astype(low)
    up_values = (
        jnp.einsum("fbd,sde->fbse", norm_two, up_low, preferred_element_type=jnp.float32).reshape(
            frame_count, frame_len, hidden_width
        )
        + up_bias
    )
    activated = gelu_tanh(up_values).astype(low)
    down_values = project(activated, down_low) + down_bias
    block_out = ((midway + gate_mlp * down_values) * row_mask).astype(low)
    upstream = cotangent.astype(jnp.float32) * row_mask
    d_gate_mlp = jnp.sum(upstream * down_values, axis=1, keepdims=True)
    d_down = (upstream * gate_mlp).astype(low)
    grad_down = jnp.einsum("fbe,fbd->ed", activated, d_down, preferred_element_type=jnp.float32)
    grad_down_bias = token_sum(d_down)
    d_activated = jnp.einsum("fbd,ed->fbe", d_down, down_low, preferred_element_type=jnp.float32)
    gelu_pull = jax.vjp(gelu_tanh, up_values)[1]
    d_up = gelu_pull(d_activated)[0].astype(low)
    d_up_parts = d_up.reshape(frame_count, frame_len, 4, model_width)
    grad_up = jnp.einsum("fbd,fbse->sde", norm_two, d_up_parts, preferred_element_type=jnp.float32)
    grad_up_bias = token_sum(d_up)
    d_norm_two = jnp.einsum("fbse,sde->fbd", d_up_parts, up_low, preferred_element_type=jnp.float32)
    second_pull = jax.vjp(modulate, midway, shift_mlp, scale_mlp)[1]
    d_midway, d_shift_mlp, d_scale_mlp = second_pull(d_norm_two)
    d_midway = d_midway + upstream
    d_gate_attn = jnp.sum(d_midway * branch, axis=1, keepdims=True)
    d_branch = (d_midway * gate_attn).astype(low)
    grad_out = jnp.einsum("fbd,fbe->de", attended, d_branch, preferred_element_type=jnp.float32)
    grad_out_bias = token_sum(d_branch)
    d_attended = jnp.einsum("fbe,de->fbd", d_branch, out_low, preferred_element_type=jnp.float32)
    d_attended = d_attended.astype(low).reshape(head_shape)
    scores = attention_scores(query_heads, key_heads, valid_slots, score_scale)
    soft = jnp.exp(scores - log_total)
    d_soft = jnp.einsum(
        "fqhs,fkhs->fhqk", d_attended, value_heads, preferred_element_type=jnp.float32
    )
    d_value_heads = jnp.einsum(
        "fhqk,fqhs->fkhs", attention, d_attended, preferred_element_type=jnp.float32
    )
    d_scores = (soft * (d_soft - jnp.sum(soft * d_soft, axis=-1, keepdims=True))).astype(low)
    d_query_heads = (
        jnp.einsum("fhqk,fkhs->fqhs", d_scores, key_heads, preferred_element_type=jnp.float32)
        * score_scale
    )
    d_key_heads = (
        jnp.einsum("fhqk,fqhs->fkhs", d_scores, query_heads, preferred_element_type=jnp.float32)
        * score_scale
    )
    flat_shape = (frame_count, frame_len, model_width)
    d_query = d_query_heads.reshape(flat_shape).astype(low)
    d_key = d_key_heads.reshape(flat_shape).astype(low)
    d_value = d_value_heads.reshape(flat_shape).astype(low)
    grad_query, grad_key, grad_value = (
        jnp.einsum("fbd,fbe->de", norm_one, member, preferred_element_type=jnp.float32)
        for member in (d_query, d_key, d_value)
    )
    grad_query_bias = token_sum(d_query)
    grad_value_bias = token_sum(d_value)
    d_norm_one = sum(
        jnp.einsum("fbe,de->fbd", member, weight, preferred_element_type=jnp.float32)
        for member, weight in ((d_query, query_low), (d_key, key_low), (d_value, value_low))
    )
    first_pull = jax.vjp(modulate, frames_f, shift_attn, scale_attn)[1]
    d_frames, d_shift_attn, d_scale_attn = first_pull(d_norm_one)
    frames_grad = (d_frames + d_midway).astype(low)
    d_modulation = jnp.concatenate(
        [d_shift_attn, d_scale_attn, d_gate_attn, d_shift_mlp, d_scale_mlp, d_gate_mlp], axis=-1
    )[:, 0, :].astype(low)
    grad_mod_bias = d_modulation[0].astype(jnp.float32)
    grad_bias = jnp.concatenate(
        [
            grad_mod_bias,
            grad_query_bias,
            grad_value_bias,
            grad_out_bias,
            grad_up_bias,
            grad_down_bias,
        ]
    )
    terms = exchange(
        jnp.concatenate(
            [
                jnp.broadcast_to(d_modulation, (count, d_modulation.shape[1])),
                grad_bias.reshape(count, -1).astype(low),
            ],
            axis=1,
        )
    )
    d_mod_all, bias_terms = terms[:, : d_modulation.shape[1]], terms[:, d_modulation.shape[1] :]

    def grouped(member, group_rows):
        member = member.astype(low).reshape(4, count // 4, 4 * rows, model_width)
        return jnp.pad(member, ((0, 0), (0, 0), (0, group_rows - 4 * rows), (0, 0)))

    group_rows = -(-4 * rows // 16) * 16
    tall_group = -(-tall_rows // 16) * 16
    a_sum, b_sum, c_sum = reduce(
        grouped(jnp.stack([grad_query, grad_key, grad_value, grad_out]), group_rows),
        grouped(grad_up, group_rows),
        jnp.pad(
            grad_down.astype(low).reshape(count // 4, 4, tall_rows, model_width),
            ((0, 0), (0, 0), (0, tall_group - tall_rows), (0, 0)),
        ),
        rows,
        (True, False, False),
    )
    red_mod = lax.dot_general(
        silu_rows, d_mod_all, (((0,), (0,)), ((), ())), preferred_element_type=jnp.float32
    )
    a_sum = a_sum.astype(jnp.float32)
    red_qkv = a_sum[:3].transpose(1, 0, 2).reshape(rows, 3 * model_width)
    red_out = a_sum[3]
    red_up = b_sum.astype(jnp.float32).transpose(1, 0, 2).reshape(rows, hidden_width)
    red_down = c_sum[:tall_rows]
    red_bias = jnp.sum(bias_terms.astype(jnp.float32), axis=0)
    d_silu = lax.dot_general(
        d_mod_all, mod_low, (((1,), (1,)), ((), ())), preferred_element_type=jnp.float32
    )
    reduced = (red_mod, red_qkv, red_out, red_up, red_down, red_bias)
    partial_sq = sum((jnp.sum(member * member) for member in reduced))
    last = exchange(
        jnp.concatenate([d_silu, jnp.broadcast_to(partial_sq, (count, 1))], axis=1)
    )
    total_sq = jnp.sum(last[:, rows])
    silu_pull = jax.vjp(silu_act, cond_f)[1]
    cond_grad = silu_pull(last[:, :rows].reshape(1, model_width))[0]
    grad_norm = jnp.sqrt(total_sq)
    factor = jnp.minimum(1.0, CLIP / (grad_norm + 1e-06))
    clipped = tuple((member * factor for member in reduced))
    masters = (mod_weight, qkv_weight, out_weight, up_weight, down_weight, biases)
    states = (mod_state, qkv_state, out_state, up_state, down_state, bias_state)
    updated = [adam_update(masters[index], states[index], clipped[index]) for index in range(6)]
    return (
        (block_out, frames_grad, cond_grad, grad_norm)
        + clipped
        + tuple(pair[0] for pair in updated)
        + tuple(pair[1] for pair in updated)
    )


def fused_shards(
    frames_in,
    conditioning,
    grid,
    cotangent,
    mod_weight,
    qkv_weight,
    out_weight,
    up_weight,
    down_weight,
    biases,
    mod_state,
    qkv_state,
    out_state,
    up_state,
    down_state,
    bias_state,
):
    frame_count, frame_len, model_width = frames_in.shape
    hidden_width = up_weight.shape[1]
    count = lax.axis_size("wide") * lax.axis_size("narrow")
    rows = mod_weight.shape[0]
    tall_rows = down_weight.shape[0]
    low = jnp.bfloat16

    def slices(member):
        return member.reshape(rows, 4, model_width).transpose(1, 0, 2)

    a_src = slices(jnp.concatenate([qkv_weight.astype(low), out_weight.astype(low)], axis=1))
    b_src = slices(up_weight.astype(low))
    cond_f = conditioning.astype(jnp.float32)
    silu_low = silu_act(cond_f).astype(low)
    mod_low = mod_weight.astype(low)
    first = exchange(
        jnp.concatenate(
            [
                silu_low.reshape(count, rows),
                jnp.broadcast_to(biases.astype(low)[None], (count, biases.shape[0])),
            ],
            axis=1,
        )
    )
    silu_rows = first[:, :rows]
    bias_f = first[:, rows:].reshape(-1).astype(jnp.float32)
    bits = count.bit_length() - 1
    crossed = [CORE, 0] + list(range(2, bits))
    sorted_rows = silu_rows.reshape((2,) * bits + (rows,)).transpose(
        [bits - 1 - bit for bit in crossed] + [bits]
    )
    terms = jnp.dot(
        sorted_rows.reshape(count, rows), mod_low, preferred_element_type=jnp.float32
    ).reshape((2,) * bits + (6 * model_width // 128, 128))
    mod_bias = bias_f[: 6 * model_width].reshape(-1, 128)
    bias_rows = bias_f[6 * model_width :].reshape(-1, model_width)
    valid_slots = slot_mask(grid, frame_len)
    row_mask = valid_slots[:, :, None].astype(jnp.float32)
    key_mask = jnp.broadcast_to(valid_slots.astype(jnp.float32), (8, frame_len))
    forward_out = forward(
        a_src, b_src, down_weight.astype(low), terms, mod_bias, bias_rows, frames_in[0], cotangent[0], key_mask, row_mask[0],
    )
    weights, mod_parts, kept, down_sums = forward_out[:3], forward_out[3], forward_out[4:-1], forward_out[-1]
    me = lax.axis_index("wide") * 2 + lax.axis_index("narrow")
    near_rows = silu_rows.reshape((2,) * bits + (rows,))
    for bit in range(bits):
        axis = bits - 1 - bit
        near_rows = jnp.where(me // (1 << bit) % 2 == 1, jnp.flip(near_rows, axis), near_rows)
    near_rows = near_rows.transpose([bits - 1 - bit for bit in reversed(SPREAD(bits))] + [bits])
    near_rows = near_rows.reshape(count, rows).T
    lift = near_rows[None, :, :, None] * jnp.eye(6, 16, dtype=low)[:, None, None, :]
    lift = lift.reshape(6, rows, 16 * count)
    block_out, frames_grad, spread, *sums, ordered, norm = backward(
        weights, mod_parts, bias_rows, down_sums, key_mask, row_mask[0], lift, mod_low, frames_in[0], cotangent[0], kept,
        rows, bits,
    )
    grads, news, news_state = update(
        sums, spread, lift, norm,
        (mod_weight, qkv_weight, out_weight, up_weight, down_weight, biases),
        (mod_state, qkv_state, out_state, up_state, down_state, bias_state),
    )
    silu_pull = jax.vjp(silu_act, cond_f)[1]
    cond_grad = silu_pull(ordered[:, :rows].reshape(1, model_width))[0]
    return (block_out[None], frames_grad[None], cond_grad, norm[0, 0]) + grads + news + news_state


def shards(*arrays):
    rows, tall_rows = arrays[4].shape[0], arrays[8].shape[0]
    fits = 4 * rows % ROUND == 0 and tall_rows % ROUND == 0
    return (fused_shards if fits else plain_shards)(*arrays)


def solution(mesh):
    tokens = P(AXES, None, None)
    matrix = P(AXES, None)
    vector = P(AXES)
    state = P(None, AXES, None)
    weights = (matrix,) * 5 + (vector,)
    states = (state,) * 5 + (P(None, AXES),)
    return jax.shard_map(
        shards,
        mesh=mesh,
        in_specs=(tokens, matrix, matrix, tokens) + weights + states,
        out_specs=(tokens, tokens, matrix, P()) + weights + weights + states,
        check_vma=False,
    )
```

profile of v0, /device:TPU:0, one launch (start us, length us, event | category | flops | bytes accessed | tf_op | source)
XLA Modules:
  0.0 357.2 jit_solution(5822972975764765627)
XLA Ops:
  0.7 0.8 convert_element_type.66
  1.5 0.7 convert_reduce_fusion
  2.2 0.1 reshape.131
  2.4 0.5 broadcast.42
  3.0 0.7 reduce.2
  3.6 0.7 reshape.142
  4.4 7.3 %all-to-all-start = ((bf16[32,2,270]{2,1,0:T(2,128)(2,1)}), bf16[32,2,270]{2,1,0:T(2,128)(2,1)S(1)}, u32[]{:S(2)}, u32[]{:S(2)}) async-start(bf16[32,2,270]{2,1,0:T(2,128)(2,1)} %reshape.142), calls=%async_computation | async-start | bytes 98304 | tf_op jit(solution)/shard_map/all_to_all | solution.py:1612
  11.8 2.1 convert_bitcast_fusion
  13.9 0.9 convert_element_type.67.mod_low
  14.8 0.6 fusion.8
  16.8 0.7 fusion.2.row_mask
  17.7 0.8 convert_element_type.63.c_src
  18.6 0.3 dot_general.8
  18.9 0.9 copy_bitcast_fusion
  19.9 0.1 reshape.143
  20.1 0.1 convert_element_type.68
  20.3 0.1 convert_element_type.69
  20.6 0.6 slice_convert_fusion.1.mod_bias
  21.2 0.6 slice_convert_fusion.bias_rows
  21.8 0.1 copy.68
  21.9 0.4 fusion
  22.3 1.0 copy.66.terms_in
  23.3 0.7 broadcast_multiply_fusion.lift
  24.1 0.6 broadcast_in_dim.9.key_mask
  24.7 150.9 %forward_gather.1 = (bf16[4,1152,1152]{2,1,0:T(8,128)(2,1)}, bf16[4,1152,1152]{2,1,0:T(8,128)(2,1)}, bf16[4608,1152]{1,0:T(8,128)(2,1)}, f32[8,1152]{1,0:T(8,128...) custom-call(bf16[4,36,1152]{2,1,0:T(8,128)(2,1)} %get-tuple-element., ...), custom_call_target="tpu_custom_call" | custom-call | flops 10000000000 | bytes 400000000 | tf_op jit(solution)/shard_map/forward_gather/pallas_call | solution.py:572
  175.5 160.0 %backward_reduce.1 = (bf16[256,1152]{1,0:T(8,128)(2,1)}, bf16[256,1152]{1,0:T(8,128)(2,1)}, bf16[512,1152]{1,0:T(8,128)(2,1)}, bf16[4,36,1152]{2,1,0:T(8,128)(2,...) custom-call(bf16[4,1152,1152]{2,1,0:T(8,128)(2,1)} %get-tuple-element.64.a_all, ...), custom_call_target="tpu_custom_call" | custom-call | flops 17999998976 | bytes 400000000 | tf_op jit(solution)/shard_map/backward_reduce/pallas_call | solution.py:1107
  335.5 1.2 slice.41
  336.7 0.8 reshape.134
  337.6 0.6 fusion.6
  338.2 17.4 %update.1 = (f32[36,6912]{1,0:T(8,128)}, f32[36,3456]{1,0:T(8,128)}, f32[36,1152]{1,0:T(8,128)}, f32[36,4608]{1,0:T(8,128)}, f32[144,1152]{1,0:T(8,128)}, /*inde...) custom-call(bf16[4,36,1152]{2,1,0:T(8,128)(2,1)} %get-tuple-element., ...), custom_call_target="tpu_custom_call" | custom-call | flops 100000000 | bytes 40000000 | tf_op jit(solution)/shard_map/update/pallas_call | solution.py:1214
  355.6 0.8 copy.86
  356.4 0.8 copy.87
  (44 shorter events, 0.8 us)
Async XLA Ops:
  0.7 13.2 %copy-start = (f32[36,6912]{1,0:T(8,128)S(1)}, f32[36,6912]{1,0:T(8,128)}, u32[]{:S(2)}) copy-start(f32[36,6912]{1,0:T(8,128)} %rest_0_.1) | copy-start | bytes 2985988
  0.7 14.1 %copy-start.9 = (s32[1,2]{1,0:T(1,128)S(1)}, s32[1,2]{1,0:T(1,128)}, u32[]{:S(2)}) copy-start(s32[1,2]{1,0:T(1,128)} %param.18) | copy-start | bytes 28
  0.7 14.8 %copy-start.5 = (f32[36,1152]{1,0:T(8,128)S(1)}, f32[36,1152]{1,0:T(8,128)}, u32[]{:S(2)}) copy-start(f32[36,1152]{1,0:T(8,128)} %rest_2_.1) | copy-start | bytes 497668
  0.7 16.8 %copy-start.3 = (f32[36,3456]{1,0:T(8,128)S(1)}, f32[36,3456]{1,0:T(8,128)}, u32[]{:S(2)}) copy-start(f32[36,3456]{1,0:T(8,128)} %rest_1_.1) | copy-start | bytes 1492996
  4.4 15.5 %all-to-all-start = ((bf16[32,2,270]{2,1,0:T(2,128)(2,1)}), bf16[32,2,270]{2,1,0:T(2,128)(2,1)S(1)}, u32[]{:S(2)}, u32[]{:S(2)}) async-start(bf16[32,2,270]{2,1,0:T(2,128)(2,1)} %reshape.142), calls=%async_computation | async-start | bytes 98304 | tf_op jit(solution)/shard_map/all_to_all | solution.py:1612
  13.9 3.8 %copy-start.2 = (f32[144,1152]{1,0:T(8,128)S(1)}, f32[144,1152]{1,0:T(8,128)}, u32[]{:S(2)}) copy-start(f32[144,1152]{1,0:T(8,128)} %rest_4_.1) | copy-start | bytes 1990660
  14.7 3.7 %copy-start.1 = (f32[36,4608]{1,0:T(8,128)S(1)}, f32[36,4608]{1,0:T(8,128)}, u32[]{:S(2)}) copy-start(f32[36,4608]{1,0:T(8,128)} %rest_3_.1) | copy-start | bytes 1990660
  17.5 1.1 copy-start.4
  175.5 162.0 %copy-start.8 = (bf16[1,1152]{1,0:T(2,128)(2,1)S(1)}, bf16[1,1152]{1,0:T(2,128)(2,1)}, u32[]{:S(2)}) copy-start(bf16[1,1152]{1,0:T(2,128)(2,1)} %param.17) | copy-start | bytes 6916
  338.2 17.4 %copy-start.7 = (bf16[256,1152]{1,0:T(8,128)(2,1)S(1)}, bf16[256,1152]{1,0:T(8,128)(2,1)}, u32[]{:S(2)}) copy-start(bf16[256,1152]{1,0:T(8,128)(2,1)} %get-tuple-element.80) | copy-start | bytes 1769476
  338.2 18.2 %copy-start.6 = (bf16[256,1152]{1,0:T(8,128)(2,1)S(1)}, bf16[256,1152]{1,0:T(8,128)(2,1)}, u32[]{:S(2)}) copy-start(bf16[256,1152]{1,0:T(8,128)(2,1)} %get-tuple-element.81) | copy-start | bytes 1769476
where the time goes:
time: 358 us; the launch traced here: 357 us
  Pallas kernels  328 us (92%)
  local copies, waits for them, and re-layouts  9.62 us (3%)
  other arithmetic  9.34 us (3%)
  starting transfers between devices  7.3 us (2%)
    pallas_call x1, Pallas kernels, backward(): pl.pallas_call(functools.partial(backward_kernel, bits, rows, tall, piece...  160 us
    pallas_call x1, Pallas kernels, forward(): pl.pallas_call(functools.partial(forward_kernel, bits, rows, pieces, cloc...  151 us
    pallas_call x1, Pallas kernels, update(): pl.pallas_call(functools.partial(update_kernel, count), out_shape=tuple(o...  17.4 us
    all_to_all x1, starting transfers between devices, exchange(): lax.all_to_all(packets, AXES, split_axis=0, concat_axis=0, tiled=True)  7.3 us
  transfers between devices with their start and end apart: 1, of which 0 were waited for; matrix products, arithmetic and copies ran while one was open for 2% of the time, Pallas kernels for 0%

commit v1 on v0

--- a/solution.py
+++ b/solution.py
@@ -98,12 +98,21 @@
         bit = other - 1
         return self.device[bit], self.quad + self.delta[bit]
 
-    def greet(self):
+    def across(self, mask):
+        wide, narrow = self.device[0][0], 1 - self.device[0][1]
+        for bit in range(self.bits):
+            if mask >> bit & 1:
+                if bit == 0:
+                    narrow = 1 - narrow
+                else:
+                    wide = wide + (1 << bit - 1) * (1 - 2 * self.digit[bit])
+        return wide, narrow
+
+    def greet(self, masks):
         barrier = pltpu.get_barrier_semaphore()
-        partners = self.device + [self.opposite]
-        for partner in partners:
-            pl.semaphore_signal(barrier, inc=1, device_id=partner, device_id_type=MESH)
-        pl.semaphore_wait(barrier, len(partners))
+        for mask in masks:
+            pl.semaphore_signal(barrier, inc=1, device_id=self.across(mask), device_id_type=MESH)
+        pl.semaphore_wait(barrier, len(masks))
 
 
 def remote(source, target, send_sem, recv_sem, device):
@@ -200,6 +209,7 @@
 
 STRIP = 32
 TILE = 384
+WIDE_TILE = 1152
 
 
 def forward_kernel(bits, rows, pieces, clock,
@@ -238,7 +248,7 @@
     own = [local(source.at[quad], stage.at[kind, quad], own_sem.at[kind]) for kind, source in enumerate((a_src, b_src))]
     own.append(local(c_src, c_block, own_sem.at[2]))
     loads = [local(terms_in, terms, load_sem.at[0]), local(frames, x_ref, load_sem.at[1])]
-    spots.greet()
+    spots.greet([1 << bit for bit in range(bits)] + [3])
     quads = []
 
     def start_quad(kind, source):
@@ -337,7 +347,7 @@
         repeat(tokens // STRIP, lambda s: body(aligned(s * STRIP, STRIP, STRIP)))
 
     def over_tiles(body):
-        repeat(width // TILE, lambda t: body(aligned(t * TILE, TILE, 128)))
+        repeat(width // WIDE_TILE, lambda t: body(aligned(t * WIDE_TILE, WIDE_TILE, 128)))
 
     pairs = {}
 
@@ -470,23 +480,30 @@
         for j in range(count // 4):
             trade(4 + j, active_turned.at[plane_rows(j, 1 - core)], other_turned.at[pl.ds(j * span, span)])
 
-    down_copies = {}
-
-    def down_gradient(j):
-        slot = j % 2
-        if j == 0:
+    def down_gradients(first_piece):
+        if first_piece == 0:
             pairs[3].wait_recv()
-        if j >= 2:
-            down_copies[j - 2].wait()
-        pairs[4 + j].wait_recv()
-
-        def body(where):
-            result = nn(active_turned[plane_rows(j, core), :], change[:, where])
-            result = result + nn(other_turned[j * span : (j + 1) * span, :], other_change[:, where])
-            down_stage[slot, :, where] = result.astype(low)
-
-        over_tiles(body)
-        down_copies[j] = local(down_stage.at[slot], down_out.at[pl.ds(j * span, span)], down_sem.at[slot])
+        for j in range(first_piece, first_piece + 4):
+            pairs[4 + j].wait_recv()
+
+        def piece(at):
+            j = first_piece + at
+            slot = remainder(j, 2)
+            target = down_out.at[aligned(j * span, span)]
+            if first_piece:
+                await_bytes(target, down_sem.at[slot])
+            else:
+                pl.when(at >= 2)(lambda: await_bytes(target, down_sem.at[slot]))
+
+            def body(where):
+                result = nn(active_turned[plane_rows(j, core), :], change[:, where])
+                result = result + nn(other_turned[aligned(j * span, span), :], other_change[:, where])
+                down_stage[slot, :, where] = result.astype(low)
+
+            repeat(width // TILE, lambda t: body(aligned(t * TILE, TILE, 128)))
+            local(down_stage.at[slot], target, down_sem.at[slot])
+
+        repeat(4, piece)
 
     takes = clock["takes"]
     agenda.step(takes["norm"], norm_first, clock["terms"][0] + clock["terms"][1] * bits)
@@ -505,23 +522,24 @@
     agenda.step(0.3, trade_active)
     agenda.step(takes["turn"], lambda: turn(attended, 1))
     agenda.step(takes["turn"], lambda: turn(second, 2))
-    for j in range(count // 4):
-        agenda.step(takes["down"], functools.partial(down_gradient, j))
+    for j in range(0, count // 4, 4):
+        agenda.step(4 * takes["down"], functools.partial(down_gradients, j))
     agenda.emit()
     finish(2)
     for done in finals:
         done()
-    for table in (slope_copies, down_copies):
-        for index in sorted(table)[-2:]:
-            table[index].wait()
+    for index in (2, 3):
+        slope_copies[index].wait()
+    for slot in range(2):
+        await_bytes(down_out.at[pl.ds(slot * span, span)], down_sem.at[slot])
 
 
 PIECES = ((0, 0, 96, False), (0, 96, 48, True), (1, 0, 96, False), (1, 96, 48, True), (2, 0, 96, False), (2, 96, 48, True))
 CLOCK = {
     "terms": (12.0, 5.0),
-    "pieces": ((8.0, 2.4), (8.0, 2.4), (16.0, 4.6), (16.0, 4.6), (24.0, 6.6), (24.0, 6.6)),
-    "settle": 3.0,
-    "takes": {"norm": 2.0, "turn": 0.6, "matmul": 2.0, "head": 0.8, "up": 3.5, "down": 1.2},
+    "pieces": ((8.0, 1.44), (8.0, 1.44), (16.0, 4.6), (16.0, 4.6), (24.0, 6.6), (24.0, 6.6)),
+    "settle": 10.0,
+    "takes": {"norm": 2.0, "turn": 0.6, "matmul": 1.8, "head": 0.42, "up": 3.0, "down": 1.0},
 }
 
 
@@ -613,10 +631,10 @@
                     block_out, frames_out, spread_out, a_out, b_out, c_out, ordered, norm_out,
                     weight, slabs, other_up, other_low, active, slope, query, key, value, x_ref, cot, change, d_attended,
                     midway, branch, down_acc, d_norm, d_midway, turned, totals, first_grads, second_grads, third_grads, recv, total,
-                    quad_block, dmod, bias_out, spread, squares, table, answers,
+                    quad_block, dmod, bias_out, spread, squares, table, answers, mine, partials,
                     weight_sem, stream_sem, load_sem, save_sem, send_sem, recv_sem, pair_send, pair_recv,
                     quad_send, quad_recv, quad_own, spread_send, spread_recv, spread_own,
-                    answer_send, answer_recv):
+                    answer_send, answer_recv, norm_send, norm_recv):
     count = 1 << bits
     spots = Spots(bits)
     core = spots.core
@@ -665,7 +683,7 @@
             )
         )
     }
-    spots.greet()
+    spots.greet([distance for distance in range(1, 8)] + [distance << 3 for distance in range(1, count // 8)])
     dmod[...] = jnp.zeros_like(dmod)
     bias_out[...] = jnp.zeros_like(bias_out)
     squares[...] = jnp.zeros_like(squares)
@@ -1007,26 +1025,53 @@
             table[t * count // 2 : (t + 1) * count // 2, 0:rows] = jnp.dot(
                 gathers, partial[t], preferred_element_type=wide, precision=lax.Precision.HIGHEST
             )
+        agenda.service(agenda.now + 0.1, functools.partial(answer_step, 0))
+
+    answer_copies = []
+
+    def answer_step(step):
+        if step:
+            slot = lax.broadcasted_iota(jnp.int32, (count, 128), 0)
+            answer_copies[step - 1].wait()
+            took = remainder(quotient(slot, 1 << step - 1), 2) == 1
+            table[...] = jnp.where(took, answers[step - 1], table[...])
+        if step < bits:
+            answer_copies.append(
+                remote(
+                    table, answers.at[step], answer_send.at[step], answer_recv.at[step], spots.device[SPREAD(bits)[step]]
+                )
+            )
+            agenda.service(agenda.now + clock["spread"], functools.partial(answer_step, step + 1))
+            return
+        for member in range(count):
+            index = spots.me
+            for place, bit in enumerate(SPREAD(bits)):
+                if member >> place & 1:
+                    index = index + spots.delta[bit]
+            ordered[pl.ds(index, 1), :] = table[member : member + 1, :]
+
+    def norm_round(first, amount, column):
+        slot = sum((1 << at) * spots.digit[first + at] for at in range(amount))
+        partials[column, slot] = mine[...]
+        copies = []
+        for distance in range(1, 1 << amount):
+            copies.append(
+                remote(
+                    mine, partials.at[column, slot], norm_send.at[column, distance], norm_recv.at[column, distance],
+                    spots.across(distance << first),
+                )
+            )
+        for copy in copies:
+            copy.wait()
+        return sum(partials[column, at] for at in range(1 << amount))
 
     def answer():
         total_square = jnp.sum(squares[...], axis=0, keepdims=True)
         folded = sum(total_square[:, at : at + 128] for at in range(0, width, 128))
-        table[count : count + 8, :] = jnp.broadcast_to(folded, (8, 128))
-        slot = lax.broadcasted_iota(jnp.int32, (count, 128), 0)
-        for step, bit in enumerate(SPREAD(bits)):
-            copy = remote(table, answers.at[step], answer_send.at[step], answer_recv.at[step], spots.device[bit])
-            copy.wait()
-            given = jnp.where(remainder(quotient(slot, 1 << step), 2) == 1, answers[step, 0:count, :], table[0:count, :])
-            summed_up = table[count : count + 8, :] + answers[step, count : count + 8, :]
-            table[0:count, :] = given
-            table[count : count + 8, :] = summed_up
-        for member in range(count):
-            index = spots.me
-            for step, bit in enumerate(SPREAD(bits)):
-                if member >> step & 1:
-                    index = index + spots.delta[bit]
-            ordered[pl.ds(index, 1), :] = table[member : member + 1, :]
-        norm_out[...] = jnp.broadcast_to(jnp.sqrt(jnp.sum(table[count : count + 8, :], axis=1, keepdims=True)), (8, 128))
+        mine[...] = jnp.broadcast_to(folded, (8, 128))
+        mine[...] = norm_round(0, 3, 0)
+        whole = norm_round(3, bits - 3, 1)
+        norm_out[...] = jnp.broadcast_to(jnp.sqrt(jnp.sum(whole, axis=1, keepdims=True)), (8, 128))
 
     spread_start = None
     takes = clock["takes"]
@@ -1099,9 +1144,10 @@
         v((2 * width, width), low), v((2 * width, width), low), v((2 * width, width), low),
         v((3, count // 2 - 1, 4 * rows, width), low), v((2, 4 * rows, width), wide), v((2, 4, rows, width), low),
         v((8, width), wide), v((8, width), wide), v((ROUND, width), low),
-        v((ROUND, width), wide), v((count + 8, 128), wide), v((bits, count + 8, 128), wide),
+        v((ROUND, width), wide), v((count, 128), wide), v((bits, count, 128), wide),
+        v((8, 128), wide), v((2, 8, 8, 128), wide),
         dma((2,)), dma((2, 2)), dma((13,)), dma((3,)), dma((kinds, count // 2)), dma((kinds, count // 2)),
-        dma((4,)), dma((4,)), dma((2, 4)), dma((2, 4)), dma((2,)), dma((bits,)), dma((bits,)), dma, dma((bits,)), dma((bits,)),
+        dma((4,)), dma((4,)), dma((2, 4)), dma((2, 4)), dma((2,)), dma((bits,)), dma((bits,)), dma, dma((bits,)), dma((bits,)), dma((2, 8)), dma((2, 8)),
     ]
     share = shaped(4, rows, width)
     return pl.pallas_call(
@@ -1171,24 +1217,25 @@
     for k in sequence:
         for copy in loads[k]:
             copy.wait()
-        tile = 128 if k == 4 else TILE
-        for part in range(w[k].shape[1] // width):
-
-            def body(t, k=k, tile=tile, part=part):
-                inner = aligned(t * tile, tile, 128)
-                where = aligned(part * width + t * tile, tile, 128)
-                if k == 0:
-                    raw = nn(lift[part, :, :half], spread[0, :, inner]) + nn(lift[part, :, half:], spread[1, :, inner])
-                elif k == 4:
-                    raw = g[4][:, where]
-                else:
-                    raw = (b_sum if k == 3 else a_sum)[3 if k == 2 else part, :, inner].astype(wide)
-                results = adam(w[k][:, where], st[k][0, :, where], st[k][1, :, where], st[k][2, :, where], raw)
-                g[k][:, where], w[k][:, where] = results[:2]
-                for slot in range(3):
-                    st[k][slot, :, where] = results[2 + slot]
-
-            repeat(width // tile, body)
+        tile = 128 if k == 4 else WIDE_TILE
+        pieces = width // tile
+
+        def body(index, k=k, tile=tile, pieces=pieces):
+            part = quotient(index, pieces)
+            inner = aligned(remainder(index, pieces) * tile, tile, 128)
+            where = aligned(index * tile, tile, 128)
+            if k == 0:
+                raw = nn(lift[part, :, :half], spread[0, :, inner]) + nn(lift[part, :, half:], spread[1, :, inner])
+            elif k == 4:
+                raw = g[4][:, where]
+            else:
+                raw = (b_sum if k == 3 else a_sum)[3 if k == 2 else part, :, inner].astype(wide)
+            results = adam(w[k][:, where], st[k][0, :, where], st[k][1, :, where], st[k][2, :, where], raw)
+            g[k][:, where], w[k][:, where] = results[:2]
+            for slot in range(3):
+                st[k][slot, :, where] = results[2 + slot]
+
+        repeat(w[k].shape[1] // tile, body)
         for at, (source, target) in enumerate(((g[k], grads[k]), (w[k], news[k]), (st[k], news_state[k]))):
             stores.append(local(source, target, out_sem.at[at, k]))
     for copy in stores:

time: 358 us -> 351 us (0.980)
  Pallas kernels: 328 us -> 322 us
    pallas_call x1, Pallas kernels: 160 us -> 155 us  [backward(): pl.pallas_call(functools.partial(backward_kernel, bits, rows, tall, piece...]
where the time goes in v1:
time: 351 us
  Pallas kernels  322 us (92%)
  local copies, waits for them, and re-layouts  9.62 us (3%)
  other arithmetic  9.34 us (3%)
  starting transfers between devices  7.3 us (2%)
    pallas_call x1, Pallas kernels, backward(): pl.pallas_call(functools.partial(backward_kernel, bits, rows, tall, piece...  155 us
    pallas_call x1, Pallas kernels, forward(): pl.pallas_call(functools.partial(forward_kernel, bits, rows, pieces, cloc...  151 us
    pallas_call x1, Pallas kernels, update(): pl.pallas_call(functools.partial(update_kernel, count), out_shape=tuple(o...  15.7 us
    all_to_all x1, starting transfers between devices, exchange(): lax.all_to_all(packets, AXES, split_axis=0, concat_axis=0, tiled=True)  7.3 us
  transfers between devices with their start and end apart: 1, of which 0 were waited for; matrix products, arithmetic and copies ran while one was open for 2% of the time, Pallas kernels for 0%

profile of v1, /device:TPU:0, one launch (start us, length us, event | category | flops | bytes accessed | tf_op | source)
XLA Modules:
  0.0 350.9 jit_solution(5600234916252865297)
XLA Ops:
  0.7 0.8 convert_element_type.66
  1.5 0.7 convert_reduce_fusion
  2.2 0.1 reshape.131
  2.4 0.5 broadcast.42
  3.0 0.7 reduce.2
  3.6 0.7 reshape.142
  4.4 7.3 %all-to-all-start = ((bf16[32,2,270]{2,1,0:T(2,128)(2,1)}), bf16[32,2,270]{2,1,0:T(2,128)(2,1)S(1)}, u32[]{:S(2)}, u32[]{:S(2)}) async-start(bf16[32,2,270]{2,1,0:T(2,128)(2,1)} %reshape.142), calls=%async_computation | async-start | bytes 98304 | tf_op jit(solution)/shard_map/all_to_all | solution.py:1659
  11.8 2.1 convert_bitcast_fusion
  13.9 0.9 convert_element_type.67.mod_low
  14.8 0.6 fusion.8
  16.8 0.7 fusion.2.row_mask
  17.7 0.8 convert_element_type.63.c_src
  18.6 0.3 dot_general.8
  18.9 0.9 copy_bitcast_fusion
  19.9 0.1 reshape.143
  20.1 0.1 convert_element_type.68
  20.3 0.1 convert_element_type.69
  20.6 0.6 slice_convert_fusion.1.mod_bias
  21.2 0.6 slice_convert_fusion.bias_rows
  21.8 0.1 copy.68
  21.9 0.4 fusion
  22.3 1.0 copy.66.terms_in
  23.3 0.7 broadcast_multiply_fusion.lift
  24.1 0.6 broadcast_in_dim.9.key_mask
  24.7 151.5 %forward_gather.1 = (bf16[4,1152,1152]{2,1,0:T(8,128)(2,1)}, bf16[4,1152,1152]{2,1,0:T(8,128)(2,1)}, bf16[4608,1152]{1,0:T(8,128)(2,1)}, f32[8,1152]{1,0:T(8,128...) custom-call(bf16[4,36,1152]{2,1,0:T(8,128)(2,1)} %get-tuple-element., ...), custom_call_target="tpu_custom_call" | custom-call | flops 10000000000 | bytes 400000000 | tf_op jit(solution)/shard_map/forward_gather/pallas_call | solution.py:590
  176.1 154.8 %backward_reduce.1 = (bf16[256,1152]{1,0:T(8,128)(2,1)}, bf16[256,1152]{1,0:T(8,128)(2,1)}, bf16[512,1152]{1,0:T(8,128)(2,1)}, bf16[4,36,1152]{2,1,0:T(8,128)(2,...) custom-call(bf16[4,1152,1152]{2,1,0:T(8,128)(2,1)} %get-tuple-element.64.a_all, ...), custom_call_target="tpu_custom_call" | custom-call | flops 17999998976 | bytes 400000000 | tf_op jit(solution)/shard_map/backward_reduce/pallas_call | solution.py:1153
  330.9 1.2 slice.41
  332.1 0.8 reshape.134
  332.9 0.6 fusion.6
  333.6 15.7 %update.1 = (f32[36,6912]{1,0:T(8,128)}, f32[36,3456]{1,0:T(8,128)}, f32[36,1152]{1,0:T(8,128)}, f32[36,4608]{1,0:T(8,128)}, f32[144,1152]{1,0:T(8,128)}, /*inde...) custom-call(bf16[4,36,1152]{2,1,0:T(8,128)(2,1)} %get-tuple-element., ...), custom_call_target="tpu_custom_call" | custom-call | flops 100000000 | bytes 40000000 | tf_op jit(solution)/shard_map/update/pallas_call | solution.py:1261
  349.3 0.8 copy.86
  350.1 0.8 copy.87
  (44 shorter events, 0.8 us)
Async XLA Ops:
  0.7 13.2 %copy-start = (f32[36,6912]{1,0:T(8,128)S(1)}, f32[36,6912]{1,0:T(8,128)}, u32[]{:S(2)}) copy-start(f32[36,6912]{1,0:T(8,128)} %rest_0_.1) | copy-start | bytes 2985988
  0.7 14.1 %copy-start.9 = (s32[1,2]{1,0:T(1,128)S(1)}, s32[1,2]{1,0:T(1,128)}, u32[]{:S(2)}) copy-start(s32[1,2]{1,0:T(1,128)} %param.18) | copy-start | bytes 28
  0.7 14.8 %copy-start.5 = (f32[36,1152]{1,0:T(8,128)S(1)}, f32[36,1152]{1,0:T(8,128)}, u32[]{:S(2)}) copy-start(f32[36,1152]{1,0:T(8,128)} %rest_2_.1) | copy-start | bytes 497668
  0.7 16.8 %copy-start.3 = (f32[36,3456]{1,0:T(8,128)S(1)}, f32[36,3456]{1,0:T(8,128)}, u32[]{:S(2)}) copy-start(f32[36,3456]{1,0:T(8,128)} %rest_1_.1) | copy-start | bytes 1492996
  4.4 15.5 %all-to-all-start = ((bf16[32,2,270]{2,1,0:T(2,128)(2,1)}), bf16[32,2,270]{2,1,0:T(2,128)(2,1)S(1)}, u32[]{:S(2)}, u32[]{:S(2)}) async-start(bf16[32,2,270]{2,1,0:T(2,128)(2,1)} %reshape.142), calls=%async_computation | async-start | bytes 98304 | tf_op jit(solution)/shard_map/all_to_all | solution.py:1659
  13.9 3.8 %copy-start.2 = (f32[144,1152]{1,0:T(8,128)S(1)}, f32[144,1152]{1,0:T(8,128)}, u32[]{:S(2)}) copy-start(f32[144,1152]{1,0:T(8,128)} %rest_4_.1) | copy-start | bytes 1990660
  14.7 3.7 %copy-start.1 = (f32[36,4608]{1,0:T(8,128)S(1)}, f32[36,4608]{1,0:T(8,128)}, u32[]{:S(2)}) copy-start(f32[36,4608]{1,0:T(8,128)} %rest_3_.1) | copy-start | bytes 1990660
  17.5 1.1 copy-start.4
  176.1 156.8 %copy-start.8 = (bf16[1,1152]{1,0:T(2,128)(2,1)S(1)}, bf16[1,1152]{1,0:T(2,128)(2,1)}, u32[]{:S(2)}) copy-start(bf16[1,1152]{1,0:T(2,128)(2,1)} %param.17) | copy-start | bytes 6916
  333.5 15.7 %copy-start.7 = (bf16[256,1152]{1,0:T(8,128)(2,1)S(1)}, bf16[256,1152]{1,0:T(8,128)(2,1)}, u32[]{:S(2)}) copy-start(bf16[256,1152]{1,0:T(8,128)(2,1)} %get-tuple-element.80) | copy-start | bytes 1769476
  333.6 16.5 %copy-start.6 = (bf16[256,1152]{1,0:T(8,128)(2,1)S(1)}, bf16[256,1152]{1,0:T(8,128)(2,1)}, u32[]{:S(2)}) copy-start(bf16[256,1152]{1,0:T(8,128)(2,1)} %get-tuple-element.81) | copy-start | bytes 1769476
